TPU v7x, 512 devices: a whole 4x8x8 slice. The times are simulated.
512 devices in a mesh: wave: 4 (over y_hi, core), tx: 8 (over z), ty: 16 (over x, y_lo).
Axes of the slice: x: 4, y: 8 (y_hi: 2, y_lo: 4; y = y_hi * 4 + y_lo), z: 8, core: 2. Of those that a mesh axis runs over, the one named last changes fastest.
Arguments:
- initial_fields: float32 [4, 2, 12, 128, 8192], P('wave', None, None, 'tx', 'ty'), may hold values from -6 to 6
- source_profiles: float32 [4, 2, 3, 8192], P('wave'), may hold values from -6 to 6
- source_waveforms: float32 [4, 2, 5], P('wave'), may hold values from -3 to 3
- material_map: int32 [128, 8192], P('tx', 'ty'), may hold values from 0 to 2
- design_density: float32 [128, 8192], P('tx', 'ty'), may hold values from 0 to 1
- material_table: float32 [3, 4], replicated, may hold values from 0.02 to 12, as said below
- plane_indices: int32 [2], replicated, may hold values from 0 to 127
- design_box: int32 [6], replicated, may hold values from 0 to 128, as said below
Outputs:
- density_gradient: float32 [128, 8192], P('tx', 'ty')
- final_electric: float32 [4, 2, 3, 128, 8192], P('wave', None, None, 'tx', 'ty')
Inputs may be any that keep to these rules, and one draw needn't show every extreme that they name: `material_map`: material ids are below 3. `material_table`: column 0 lies in [1, 12], column 1 in [0.5, 3], column 2 in [0.3, 1.5], column 3 in [0.02, 0.5]. `plane_indices`: entry 0 is the source plane of the forward run, entry 1 the monitor plane where the adjoint run's source enters. `design_box`: x0 <= 16, y0 <= 16, x1 = 128, y1 = 128, z0 = 0, z1 = 64.
All inputs are finite; a program needn't handle non-finite values.
Results may differ from a plain program's by a relative error of at most 0.0001.
Values sent between devices are 32-bit elements; how exact they have to be, the bound alone decides.
A program may use at most 64 MiB of HBM per device.

v0:
```python
import jax
import jax.numpy as jnp
from jax import lax
from jax.sharding import PartitionSpec as P

NZ = 64
STEPS = 5
NMAT = 3


time_step = 0.5
contrast = 2.0


def shifted_2(value, axis, steps):
    count = lax.axis_size(axis)
    initial, last = (max(0, -steps), min(count, count - steps))
    return lax.ppermute(value, axis, [(source, source + steps) for source in range(initial, last)])


def ahead_rows(values, border):
    return jnp.concatenate([values[:, 1:], border], axis=1)


def behind_rows(values, border):
    return jnp.concatenate([border, values[:, :-1]], axis=1)


def ahead_lines(values, border):
    width = border.shape[2]
    return jnp.concatenate([values[:, :, width:], border], axis=2)


def behind_lines(values, border):
    width = border.shape[2]
    return jnp.concatenate([border, values[:, :, :-width]], axis=2)


def ahead_depth(values, depth_last):
    shifted = jnp.concatenate([values[:, :, 1:], jnp.zeros_like(values[:, :, :1])], axis=2)
    return jnp.where(depth_last, 0.0, shifted)


def behind_depth(values, depth_first):
    shifted = jnp.concatenate([jnp.zeros_like(values[:, :, :1]), values[:, :, :-1]], axis=2)
    return jnp.where(depth_first, 0.0, shifted)


def curl_electric(field, rows_ahead, lines_ahead, depth_last):
    part_one, part_two, part_three = (field[:, 0], field[:, 1], field[:, 2])
    curl_one = (
        ahead_lines(part_three, lines_ahead[:, 1])
        - part_three
        - (ahead_depth(part_two, depth_last) - part_two)
    )
    curl_two = (
        ahead_depth(part_one, depth_last)
        - part_one
        - (ahead_rows(part_three, rows_ahead[:, 1]) - part_three)
    )
    curl_three = (
        ahead_rows(part_two, rows_ahead[:, 0])
        - part_two
        - (ahead_lines(part_one, lines_ahead[:, 0]) - part_one)
    )
    return jnp.stack([curl_one, curl_two, curl_three], axis=1)


def curl_magnetic(field, rows_behind, lines_behind, depth_first):
    part_one, part_two, part_three = (field[:, 0], field[:, 1], field[:, 2])
    curl_one = (
        part_three
        - behind_lines(part_three, lines_behind[:, 1])
        - (part_two - behind_depth(part_two, depth_first))
    )
    curl_two = (
        part_one
        - behind_depth(part_one, depth_first)
        - (part_three - behind_rows(part_three, rows_behind[:, 1]))
    )
    curl_three = (
        part_two
        - behind_rows(part_two, rows_behind[:, 0])
        - (part_one - behind_lines(part_one, lines_behind[:, 0]))
    )
    return jnp.stack([curl_one, curl_two, curl_three], axis=1)


def electric_borders(field):
    rows_ahead = shifted_2(field[:, 1:, :1, :], "tx", -1)
    flat_part = field[:, 0::2, :, :NZ].reshape(field.shape[0], 2, field.shape[2] * NZ)
    lines_ahead = shifted_2(flat_part, "ty", -1)
    return (rows_ahead, lines_ahead.reshape(field.shape[0], 2, field.shape[2], NZ))


def magnetic_borders(field):
    rows_behind = shifted_2(field[:, 1:, -1:, :], "tx", 1)
    flat_part = field[:, 0::2, :, -NZ:].reshape(field.shape[0], 2, field.shape[2] * NZ)
    lines_behind = shifted_2(flat_part, "ty", 1)
    return (rows_behind, lines_behind.reshape(field.shape[0], 2, field.shape[2], NZ))


def design_mask(grid_rows, grid_flat, design_box):
    lines = grid_flat // NZ
    depth_ids = grid_flat % NZ
    in_rows = (grid_rows >= design_box[0]) & (grid_rows < design_box[1])
    in_lines = (
        (lines >= design_box[2])
        & (lines < design_box[3])
        & (depth_ids >= design_box[4])
        & (depth_ids < design_box[5])
    )
    return (in_rows[:, None] & in_lines[None, :]).astype(jnp.float32)


def coefficients(material_map, design_density, material_table, inside_design):
    damping = material_table[:, 3]
    denom = 1.0 + 0.25 * damping
    decay = (1.0 - 0.25 * damping) / denom
    drive = material_table[:, 2] * material_table[:, 2] * time_step / denom
    coupled = drive * material_table[:, 1]
    permittivity = jnp.zeros(material_map.shape, jnp.float32)
    decay_map = jnp.zeros(material_map.shape, jnp.float32)
    drive_map = jnp.zeros(material_map.shape, jnp.float32)
    coupled_map = jnp.zeros(material_map.shape, jnp.float32)
    for material_id in range(NMAT):
        chosen = (material_map == material_id).astype(jnp.float32)
        permittivity = permittivity + chosen * material_table[material_id, 0]
        decay_map = decay_map + chosen * decay[material_id]
        drive_map = drive_map + chosen * drive[material_id]
        coupled_map = coupled_map + chosen * coupled[material_id]
    permittivity = permittivity + inside_design * design_density * contrast
    return jnp.stack([time_step / permittivity, decay_map, drive_map, coupled_map])


def advance(
    electric,
    magnetic,
    polarization,
    current,
    coeffs,
    inside,
    depth_last,
    depth_first,
    source,
    get_electric,
    get_magnetic,
):
    rows_ahead, lines_ahead = get_electric(electric)
    magnetic = (
        magnetic - time_step * curl_electric(electric, rows_ahead, lines_ahead, depth_last)
    ) * inside
    current = coeffs[1] * current + coeffs[3] * electric - coeffs[2] * polarization
    polarization = polarization + time_step * current
    rows_behind, lines_behind = get_magnetic(magnetic)
    electric = electric + coeffs[0] * (
        curl_magnetic(magnetic, rows_behind, lines_behind, depth_first) - current - source
    )
    return (electric, magnetic, polarization, current)


def on_device(
    initial_fields,
    source_profiles,
    source_waveforms,
    material_map,
    design_density,
    material_table,
    plane_indices,
    design_box,
):
    rows_here, flat_here = material_map.shape
    tile_row = lax.axis_index("tx")
    tile_col = lax.axis_index("ty")
    grid_rows = tile_row * rows_here + jnp.arange(rows_here, dtype=jnp.int32)
    grid_flat = tile_col * flat_here + jnp.arange(flat_here, dtype=jnp.int32)
    inside_design = design_mask(grid_rows, grid_flat, design_box)
    coeffs = coefficients(material_map, design_density, material_table, inside_design)
    fields = initial_fields[0]
    profiles = source_profiles[0]
    waveforms = source_waveforms[0]
    inside = 1.0
    profiles_here = lax.dynamic_slice_in_dim(profiles, tile_col * flat_here, flat_here, axis=2)
    depth_ids = grid_flat % NZ
    depth_last = depth_ids == NZ - 1
    depth_first = depth_ids == 0
    plane_rows = (grid_rows[None, :] == plane_indices[:, None]).astype(jnp.float32)
    electric = fields[:, 0:3]
    magnetic = fields[:, 3:6]
    polarization = fields[:, 6:9]
    current = fields[:, 9:12]
    forward_history = [electric[0]]
    adjoint_history = [electric[1]]
    for step_index in range(STEPS):
        source = (
            waveforms[:, step_index][:, None, None, None]
            * profiles_here[:, :, None, :]
            * plane_rows[:, None, :, None]
        )
        electric, magnetic, polarization, current = advance(
            electric,
            magnetic,
            polarization,
            current,
            coeffs,
            inside,
            depth_last,
            depth_first,
            source,
            electric_borders,
            magnetic_borders,
        )
        forward_history.append(electric[0])
        adjoint_history.append(electric[1])
    partial_value = jnp.zeros((rows_here, flat_here), jnp.float32)
    for pair_index in range(1, STEPS + 1):
        partial_value = partial_value + jnp.sum(
            adjoint_history[STEPS + 1 - pair_index]
            * (forward_history[pair_index] - forward_history[pair_index - 1]),
            axis=0,
        )
    collected = lax.psum(partial_value, "wave")
    density_gradient = contrast * inside_design * collected
    return (density_gradient, electric[None])


def solution(mesh):
    placed = (
        P("wave", None, None, "tx", "ty"),
        P("wave", None, None, None),
        P("wave", None, None),
        P("tx", "ty"),
        P("tx", "ty"),
        P(),
        P(),
        P(),
    )
    return jax.shard_map(
        on_device,
        mesh=mesh,
        in_specs=placed,
        out_specs=(P("tx", "ty"), P("wave", None, None, "tx", "ty")),
        check_vma=False,
    )
```

profile of v0, /device:TPU:272, one launch (start us, length us, event | category | flops | bytes accessed | tf_op | source)
XLA Modules:
  0.0 151.1 jit_solution(15769013824842356531)
XLA Ops:
  2.0 2.4 %collective-permute-start = (f32[2,2,1024]{2,0,1:T(2,128)S(1)}, f32[2,2,1024]{2,0,1:T(2,128)S(1)}, u32[]{:S(2)}, u32[]{:S(2)}) collective-permute-start(f32[2,2,1024]{2,0,1:T(2,128)S(1)} %reshape.295), channel_id=1, source_target_pairs={{1,0},{2,1},{3,2},{4,3},{5,4},{6,5},{7,6},{8,7},{9,8},{10,9},{11,1... | collective-permute-start | bytes 49160 | tf_op jit(solution)/shard_map/ppermute | solution.py:18
  11.8 2.5 %compare_and_fusion = pred[512]{0:T(512)(128)(4,1)S(1)} fusion(s32[]{:T(128)} %bitcast.5, s32[]{:T(128)} %bitcast.4, s32[]{:T(128)} %bitcast.3, s32[]{:T(128)} %bitcast.2, s32[]{:T(128)S(6)} %mul.416), kind=kLoop, calls=%fused_computation.258 | loop fusion | flops 13824 | bytes 532 | tf_op jit(solution)/shard_map/and | solution.py:108
  17.7 5.7 %select_add_fusion.2 = (f32[16,512]{1,0:T(8,128)S(1)}, f32[16,512]{1,0:T(8,128)S(1)}, f32[16,512]{1,0:T(8,128)S(1)}) fusion(pred[16,512]{1,0:T(8,128)(4,1)S(1)} %get-tuple-element.20, pred[16,512]{1,0:T(8,128)(4,1)S(1)} %get-tuple-element.19, pred[16,512]{1,0:T(8,128)(4,1)S(1)} %get-tuple-element.18, f32[]{:T(128)} %bitcast.30, f32[]{:T(128)} %bitcast.29, ...), kind=kLoop, calls=%fused_computation.212 | loop fusion | flops 122880 | bytes 122916 | tf_op jit(solution)/shard_map/add | solution.py:129
  24.3 3.5 %collective-permute-start.2 = (f32[2,2,1024]{2,0,1:T(2,128)S(1)}, f32[2,2,1024]{2,0,1:T(2,128)S(1)}, u32[]{:S(2)}, u32[]{:S(2)}) collective-permute-start(f32[2,2,1024]{2,0,1:T(2,128)S(1)} %reshape.297), channel_id=1, source_target_pairs={{0,1},{1,2},{2,3},{3,4},{4,5},{5,6},{6,7},{7,8},{8,9},{9,10},{10,1... | collective-permute-start | bytes 49160 | tf_op jit(solution)/shard_map/ppermute | solution.py:18
  27.8 3.9 %collective-permute-start.3 = (f32[2,2,1,512]{3,2,0,1:T(1,128)S(1)}, f32[2,2,1,512]{3,2,0,1:T(1,128)S(1)}, u32[]{:S(2)}, u32[]{:S(2)}) collective-permute-start(f32[2,2,1,512]{3,2,0,1:T(1,128)S(1)} %slice.802), channel_id=1, source_target_pairs={{0,16},{16,32},{32,48},{48,64},{64,80},{80,96},{96,112},{1,17},{17... | collective-permute-start | bytes 24584 | tf_op jit(solution)/shard_map/ppermute | solution.py:18
  31.8 2.8 %collective-permute-done.3 = f32[2,2,1,512]{3,2,0,1:T(1,128)S(1)} collective-permute-done((f32[2,2,1,512]{3,2,0,1:T(1,128)S(1)}, f32[2,2,1,512]{3,2,0,1:T(1,128)S(1)}, u32[]{:S(2)}, u32[]{:S(2)}) %collective-permute-start.3) | collective-permute-done | bytes 8224 | tf_op jit(solution)/shard_map/ppermute | solution.py:18
  37.4 2.4 %collective-permute-start.4 = (f32[2,2,1024]{2,0,1:T(2,128)S(1)}, f32[2,2,1024]{2,0,1:T(2,128)S(1)}, u32[]{:S(2)}, u32[]{:S(2)}) collective-permute-start(f32[2,2,1024]{2,0,1:T(2,128)S(1)} %copy.82), channel_id=1, source_target_pairs={{1,0},{2,1},{3,2},{4,3},{5,4},{6,5},{7,6},{8,7},{9,8},{10,9},{11,1... | collective-permute-start | bytes 49160 | tf_op jit(solution)/shard_map/ppermute | solution.py:18
  40.7 4.6 %collective-permute-done.4 = f32[2,2,1024]{2,0,1:T(2,128)S(1)} collective-permute-done((f32[2,2,1024]{2,0,1:T(2,128)S(1)}, f32[2,2,1024]{2,0,1:T(2,128)S(1)}, u32[]{:S(2)}, u32[]{:S(2)}) %collective-permute-start.4) | collective-permute-done | bytes 16416 | tf_op jit(solution)/shard_map/ppermute | solution.py:18
  45.9 6.6 %collective-permute-start.6 = (f32[2,2,1024]{2,0,1:T(2,128)S(1)}, f32[2,2,1024]{2,0,1:T(2,128)S(1)}, u32[]{:S(2)}, u32[]{:S(2)}) collective-permute-start(f32[2,2,1024]{2,0,1:T(2,128)S(1)} %reshape.301), channel_id=1, source_target_pairs={{0,1},{1,2},{2,3},{3,4},{4,5},{5,6},{6,7},{7,8},{8,9},{9,10},{10,1... | collective-permute-start | bytes 49160 | tf_op jit(solution)/shard_map/ppermute | solution.py:18
  52.5 4.0 %collective-permute-start.7 = (f32[2,2,1,512]{3,2,0,1:T(1,128)S(1)}, f32[2,2,1,512]{3,2,0,1:T(1,128)S(1)}, u32[]{:S(2)}, u32[]{:S(2)}) collective-permute-start(f32[2,2,1,512]{3,2,0,1:T(1,128)S(1)} %slice.832), channel_id=1, source_target_pairs={{0,16},{16,32},{32,48},{48,64},{64,80},{80,96},{96,112},{1,17},{17... | collective-permute-start | bytes 24584 | tf_op jit(solution)/shard_map/ppermute | solution.py:18
  56.5 2.7 %collective-permute-done.7 = f32[2,2,1,512]{3,2,0,1:T(1,128)S(1)} collective-permute-done((f32[2,2,1,512]{3,2,0,1:T(1,128)S(1)}, f32[2,2,1,512]{3,2,0,1:T(1,128)S(1)}, u32[]{:S(2)}, u32[]{:S(2)}) %collective-permute-start.7) | collective-permute-done | bytes 8224 | tf_op jit(solution)/shard_map/ppermute | solution.py:18
  65.5 2.4 %collective-permute-done.8 = f32[2,2,1024]{2,0,1:T(2,128)S(1)} collective-permute-done((f32[2,2,1024]{2,0,1:T(2,128)S(1)}, f32[2,2,1024]{2,0,1:T(2,128)S(1)}, u32[]{:S(2)}, u32[]{:S(2)}) %collective-permute-start.8) | collective-permute-done | bytes 16416 | tf_op jit(solution)/shard_map/ppermute | solution.py:18
  68.5 4.6 %collective-permute-start.10 = (f32[2,2,1024]{2,0,1:T(2,128)S(1)}, f32[2,2,1024]{2,0,1:T(2,128)S(1)}, u32[]{:S(2)}, u32[]{:S(2)}) collective-permute-start(f32[2,2,1024]{2,0,1:T(2,128)S(1)} %reshape.305), channel_id=1, source_target_pairs={{0,1},{1,2},{2,3},{3,4},{4,5},{5,6},{6,7},{7,8},{8,9},{9,10},{10,1... | collective-permute-start | bytes 49160 | tf_op jit(solution)/shard_map/ppermute | solution.py:18
  73.1 3.9 %collective-permute-start.11 = (f32[2,2,1,512]{3,2,0,1:T(1,128)S(1)}, f32[2,2,1,512]{3,2,0,1:T(1,128)S(1)}, u32[]{:S(2)}, u32[]{:S(2)}) collective-permute-start(f32[2,2,1,512]{3,2,0,1:T(1,128)S(1)} %slice.860), channel_id=1, source_target_pairs={{0,16},{16,32},{32,48},{48,64},{64,80},{80,96},{96,112},{1,17},{17... | collective-permute-start | bytes 24584 | tf_op jit(solution)/shard_map/ppermute | solution.py:18
  77.0 2.8 %collective-permute-done.11 = f32[2,2,1,512]{3,2,0,1:T(1,128)S(1)} collective-permute-done((f32[2,2,1,512]{3,2,0,1:T(1,128)S(1)}, f32[2,2,1,512]{3,2,0,1:T(1,128)S(1)}, u32[]{:S(2)}, u32[]{:S(2)}) %collective-permute-start.11) | collective-permute-done | bytes 8224 | tf_op jit(solution)/shard_map/ppermute | solution.py:18
  86.0 2.5 %collective-permute-done.12 = f32[2,2,1024]{2,0,1:T(2,128)S(1)} collective-permute-done((f32[2,2,1024]{2,0,1:T(2,128)S(1)}, f32[2,2,1024]{2,0,1:T(2,128)S(1)}, u32[]{:S(2)}, u32[]{:S(2)}) %collective-permute-start.12) | collective-permute-done | bytes 16416 | tf_op jit(solution)/shard_map/ppermute | solution.py:18
  89.7 4.6 %collective-permute-start.14 = (f32[2,2,1024]{2,0,1:T(2,128)S(1)}, f32[2,2,1024]{2,0,1:T(2,128)S(1)}, u32[]{:S(2)}, u32[]{:S(2)}) collective-permute-start(f32[2,2,1024]{2,0,1:T(2,128)S(1)} %reshape.309), channel_id=1, source_target_pairs={{0,1},{1,2},{2,3},{3,4},{4,5},{5,6},{6,7},{7,8},{8,9},{9,10},{10,1... | collective-permute-start | bytes 49160 | tf_op jit(solution)/shard_map/ppermute | solution.py:18
  94.3 3.9 %collective-permute-start.15 = (f32[2,2,1,512]{3,2,0,1:T(1,128)S(1)}, f32[2,2,1,512]{3,2,0,1:T(1,128)S(1)}, u32[]{:S(2)}, u32[]{:S(2)}) collective-permute-start(f32[2,2,1,512]{3,2,0,1:T(1,128)S(1)} %slice.888), channel_id=1, source_target_pairs={{0,16},{16,32},{32,48},{48,64},{64,80},{80,96},{96,112},{1,17},{17... | collective-permute-start | bytes 24584 | tf_op jit(solution)/shard_map/ppermute | solution.py:18
  98.2 2.8 %collective-permute-done.15 = f32[2,2,1,512]{3,2,0,1:T(1,128)S(1)} collective-permute-done((f32[2,2,1,512]{3,2,0,1:T(1,128)S(1)}, f32[2,2,1,512]{3,2,0,1:T(1,128)S(1)}, u32[]{:S(2)}, u32[]{:S(2)}) %collective-permute-start.15) | collective-permute-done | bytes 8224 | tf_op jit(solution)/shard_map/ppermute | solution.py:18
  112.1 2.4 %collective-permute-done.16 = f32[2,2,1024]{2,0,1:T(2,128)S(1)} collective-permute-done((f32[2,2,1024]{2,0,1:T(2,128)S(1)}, f32[2,2,1024]{2,0,1:T(2,128)S(1)}, u32[]{:S(2)}, u32[]{:S(2)}) %collective-permute-start.16) | collective-permute-done | bytes 16416 | tf_op jit(solution)/shard_map/ppermute | solution.py:18
  118.4 4.6 %collective-permute-start.18 = (f32[2,2,1024]{2,0,1:T(2,128)S(1)}, f32[2,2,1024]{2,0,1:T(2,128)S(1)}, u32[]{:S(2)}, u32[]{:S(2)}) collective-permute-start(f32[2,2,1024]{2,0,1:T(2,128)S(1)} %copy.127), channel_id=1, source_target_pairs={{0,1},{1,2},{2,3},{3,4},{4,5},{5,6},{6,7},{7,8},{8,9},{9,10},{10,1... | collective-permute-start | bytes 49160 | tf_op jit(solution)/shard_map/ppermute | solution.py:18
  123.1 3.9 %collective-permute-start.19 = (f32[2,2,1,512]{3,2,1,0:T(1,128)S(1)}, f32[2,2,1,512]{3,2,1,0:T(1,128)S(1)}, u32[]{:S(2)}, u32[]{:S(2)}) collective-permute-start(f32[2,2,1,512]{3,2,1,0:T(1,128)S(1)} %slice.916), channel_id=1, source_target_pairs={{0,16},{16,32},{32,48},{48,64},{64,80},{80,96},{96,112},{1,17},{17... | collective-permute-start | bytes 24584 | tf_op jit(solution)/shard_map/ppermute | solution.py:18
  127.0 2.8 %collective-permute-done.19 = f32[2,2,1,512]{3,2,1,0:T(1,128)S(1)} collective-permute-done((f32[2,2,1,512]{3,2,1,0:T(1,128)S(1)}, f32[2,2,1,512]{3,2,1,0:T(1,128)S(1)}, u32[]{:S(2)}, u32[]{:S(2)}) %collective-permute-start.19) | collective-permute-done | bytes 8224 | tf_op jit(solution)/shard_map/ppermute | solution.py:18
  132.3 18.1 %psum.7 = f32[16,512]{1,0:T(8,128)S(1)} all-reduce(f32[16,512]{1,0:T(8,128)S(1)} %add_add_fusion), channel_id=1, replica_groups=mesh['wave'=4,'tx'=8,'ty'=16] {'wave'}, use_global_device_ids=true, to_apply=%region_5.6 | all-reduce | flops 8192 | bytes 65536 | tf_op jit(solution)/shard_map/psum | solution.py:222
  (244 shorter events, 49.0 us)
Async XLA Ops:
  2.0 21.7 %collective-permute-start = (f32[2,2,1024]{2,0,1:T(2,128)S(1)}, f32[2,2,1024]{2,0,1:T(2,128)S(1)}, u32[]{:S(2)}, u32[]{:S(2)}) collective-permute-start(f32[2,2,1024]{2,0,1:T(2,128)S(1)} %reshape.295), channel_id=1, source_target_pairs={{1,0},{2,1},{3,2},{4,3},{5,4},{6,5},{7,6},{8,7},{9,8},{10,9},{11,1... | collective-permute-start | bytes 49160 | tf_op jit(solution)/shard_map/ppermute | solution.py:18
  4.3 19.2 %collective-permute-start.1 = (f32[2,2,1,512]{3,2,0,1:T(1,128)S(1)}, f32[2,2,1,512]{3,2,0,1:T(1,128)S(1)}, u32[]{:S(2)}, u32[]{:S(2)}) collective-permute-start(f32[2,2,1,512]{3,2,0,1:T(1,128)S(1)} %slice.789), channel_id=1, source_target_pairs={{16,0},{32,16},{48,32},{64,48},{80,64},{96,80},{112,96},{17,1},{33... | collective-permute-start | bytes 24584 | tf_op jit(solution)/shard_map/ppermute | solution.py:18
  8.9 79.7 %copy-start.16 = (pred[512]{0:T(512)(128)(4,1)}, pred[512]{0:T(512)(128)(4,1)S(1)}, u32[]{:S(2)}) copy-start(pred[512]{0:T(512)(128)(4,1)S(1)} %broadcast_compare_fusion.3) | copy-start | bytes 1540
  11.8 90.2 %copy-start.7 = (f32[2,16]{1,0:T(2,128)}, f32[2,16]{1,0:T(2,128)S(1)}, u32[]{:S(2)}) copy-start(f32[2,16]{1,0:T(2,128)S(1)} %compare_convert_fusion) | copy-start | bytes 388
  23.4 56.7 %copy-start.18 = (pred[512]{0:T(512)(128)(4,1)}, pred[512]{0:T(512)(128)(4,1)S(1)}, u32[]{:S(2)}) copy-start(pred[512]{0:T(512)(128)(4,1)S(1)} %broadcast_compare_fusion.4) | copy-start | bytes 1540
  24.3 10.3 %collective-permute-start.2 = (f32[2,2,1024]{2,0,1:T(2,128)S(1)}, f32[2,2,1024]{2,0,1:T(2,128)S(1)}, u32[]{:S(2)}, u32[]{:S(2)}) collective-permute-start(f32[2,2,1024]{2,0,1:T(2,128)S(1)} %reshape.297), channel_id=1, source_target_pairs={{0,1},{1,2},{2,3},{3,4},{4,5},{5,6},{6,7},{7,8},{8,9},{9,10},{10,1... | collective-permute-start | bytes 49160 | tf_op jit(solution)/shard_map/ppermute | solution.py:18
  27.8 6.8 %collective-permute-start.3 = (f32[2,2,1,512]{3,2,0,1:T(1,128)S(1)}, f32[2,2,1,512]{3,2,0,1:T(1,128)S(1)}, u32[]{:S(2)}, u32[]{:S(2)}) collective-permute-start(f32[2,2,1,512]{3,2,0,1:T(1,128)S(1)} %slice.802), channel_id=1, source_target_pairs={{0,16},{16,32},{32,48},{48,64},{64,80},{80,96},{96,112},{1,17},{17... | collective-permute-start | bytes 24584 | tf_op jit(solution)/shard_map/ppermute | solution.py:18
  35.1 5.5 %collective-permute-start.5 = (f32[2,2,1,512]{3,1,2,0:T(2,128)S(1)}, f32[2,2,1,512]{3,1,2,0:T(2,128)S(1)}, u32[]{:S(2)}, u32[]{:S(2)}) collective-permute-start(f32[2,2,1,512]{3,1,2,0:T(2,128)S(1)} %copy.139), channel_id=1, source_target_pairs={{16,0},{32,16},{48,32},{64,48},{80,64},{96,80},{112,96},{17,1},{33... | collective-permute-start | bytes 24584 | tf_op jit(solution)/shard_map/ppermute | solution.py:18
  37.4 7.9 %collective-permute-start.4 = (f32[2,2,1024]{2,0,1:T(2,128)S(1)}, f32[2,2,1024]{2,0,1:T(2,128)S(1)}, u32[]{:S(2)}, u32[]{:S(2)}) collective-permute-start(f32[2,2,1024]{2,0,1:T(2,128)S(1)} %copy.82), channel_id=1, source_target_pairs={{1,0},{2,1},{3,2},{4,3},{5,4},{6,5},{7,6},{8,7},{9,8},{10,9},{11,1... | collective-permute-start | bytes 49160 | tf_op jit(solution)/shard_map/ppermute | solution.py:18
  45.9 13.4 %collective-permute-start.6 = (f32[2,2,1024]{2,0,1:T(2,128)S(1)}, f32[2,2,1024]{2,0,1:T(2,128)S(1)}, u32[]{:S(2)}, u32[]{:S(2)}) collective-permute-start(f32[2,2,1024]{2,0,1:T(2,128)S(1)} %reshape.301), channel_id=1, source_target_pairs={{0,1},{1,2},{2,3},{3,4},{4,5},{5,6},{6,7},{7,8},{8,9},{9,10},{10,1... | collective-permute-start | bytes 49160 | tf_op jit(solution)/shard_map/ppermute | solution.py:18
  52.5 6.8 %collective-permute-start.7 = (f32[2,2,1,512]{3,2,0,1:T(1,128)S(1)}, f32[2,2,1,512]{3,2,0,1:T(1,128)S(1)}, u32[]{:S(2)}, u32[]{:S(2)}) collective-permute-start(f32[2,2,1,512]{3,2,0,1:T(1,128)S(1)} %slice.832), channel_id=1, source_target_pairs={{0,16},{16,32},{32,48},{48,64},{64,80},{80,96},{96,112},{1,17},{17... | collective-permute-start | bytes 24584 | tf_op jit(solution)/shard_map/ppermute | solution.py:18
  59.9 5.5 %collective-permute-start.9 = (f32[2,2,1,512]{3,2,0,1:T(1,128)S(1)}, f32[2,2,1,512]{3,2,0,1:T(1,128)S(1)}, u32[]{:S(2)}, u32[]{:S(2)}) collective-permute-start(f32[2,2,1,512]{3,2,0,1:T(1,128)S(1)} %slice.847), channel_id=1, source_target_pairs={{16,0},{32,16},{48,32},{64,48},{80,64},{96,80},{112,96},{17,1},{33... | collective-permute-start | bytes 24584 | tf_op jit(solution)/shard_map/ppermute | solution.py:18
  62.2 5.6 %collective-permute-start.8 = (f32[2,2,1024]{2,0,1:T(2,128)S(1)}, f32[2,2,1024]{2,0,1:T(2,128)S(1)}, u32[]{:S(2)}, u32[]{:S(2)}) collective-permute-start(f32[2,2,1024]{2,0,1:T(2,128)S(1)} %copy.95), channel_id=1, source_target_pairs={{1,0},{2,1},{3,2},{4,3},{5,4},{6,5},{7,6},{8,7},{9,8},{10,9},{11,1... | collective-permute-start | bytes 49160 | tf_op jit(solution)/shard_map/ppermute | solution.py:18
  68.5 11.4 %collective-permute-start.10 = (f32[2,2,1024]{2,0,1:T(2,128)S(1)}, f32[2,2,1024]{2,0,1:T(2,128)S(1)}, u32[]{:S(2)}, u32[]{:S(2)}) collective-permute-start(f32[2,2,1024]{2,0,1:T(2,128)S(1)} %reshape.305), channel_id=1, source_target_pairs={{0,1},{1,2},{2,3},{3,4},{4,5},{5,6},{6,7},{7,8},{8,9},{9,10},{10,1... | collective-permute-start | bytes 49160 | tf_op jit(solution)/shard_map/ppermute | solution.py:18
  73.1 6.8 %collective-permute-start.11 = (f32[2,2,1,512]{3,2,0,1:T(1,128)S(1)}, f32[2,2,1,512]{3,2,0,1:T(1,128)S(1)}, u32[]{:S(2)}, u32[]{:S(2)}) collective-permute-start(f32[2,2,1,512]{3,2,0,1:T(1,128)S(1)} %slice.860), channel_id=1, source_target_pairs={{0,16},{16,32},{32,48},{48,64},{64,80},{80,96},{96,112},{1,17},{17... | collective-permute-start | bytes 24584 | tf_op jit(solution)/shard_map/ppermute | solution.py:18
  80.4 5.5 %collective-permute-start.13 = (f32[2,2,1,512]{3,1,2,0:T(2,128)S(1)}, f32[2,2,1,512]{3,1,2,0:T(2,128)S(1)}, u32[]{:S(2)}, u32[]{:S(2)}) collective-permute-start(f32[2,2,1,512]{3,1,2,0:T(2,128)S(1)} %copy.143), channel_id=1, source_target_pairs={{16,0},{32,16},{48,32},{64,48},{80,64},{96,80},{112,96},{17,1},{33... | collective-permute-start | bytes 24584 | tf_op jit(solution)/shard_map/ppermute | solution.py:18
  82.8 5.6 %collective-permute-start.12 = (f32[2,2,1024]{2,0,1:T(2,128)S(1)}, f32[2,2,1024]{2,0,1:T(2,128)S(1)}, u32[]{:S(2)}, u32[]{:S(2)}) collective-permute-start(f32[2,2,1024]{2,0,1:T(2,128)S(1)} %copy.107), channel_id=1, source_target_pairs={{1,0},{2,1},{3,2},{4,3},{5,4},{6,5},{7,6},{8,7},{9,8},{10,9},{11,1... | collective-permute-start | bytes 49160 | tf_op jit(solution)/shard_map/ppermute | solution.py:18
  89.7 11.4 %collective-permute-start.14 = (f32[2,2,1024]{2,0,1:T(2,128)S(1)}, f32[2,2,1024]{2,0,1:T(2,128)S(1)}, u32[]{:S(2)}, u32[]{:S(2)}) collective-permute-start(f32[2,2,1024]{2,0,1:T(2,128)S(1)} %reshape.309), channel_id=1, source_target_pairs={{0,1},{1,2},{2,3},{3,4},{4,5},{5,6},{6,7},{7,8},{8,9},{9,10},{10,1... | collective-permute-start | bytes 49160 | tf_op jit(solution)/shard_map/ppermute | solution.py:18
  94.3 6.8 %collective-permute-start.15 = (f32[2,2,1,512]{3,2,0,1:T(1,128)S(1)}, f32[2,2,1,512]{3,2,0,1:T(1,128)S(1)}, u32[]{:S(2)}, u32[]{:S(2)}) collective-permute-start(f32[2,2,1,512]{3,2,0,1:T(1,128)S(1)} %slice.888), channel_id=1, source_target_pairs={{0,16},{16,32},{32,48},{48,64},{64,80},{80,96},{96,112},{1,17},{17... | collective-permute-start | bytes 24584 | tf_op jit(solution)/shard_map/ppermute | solution.py:18
  103.5 7.4 %collective-permute-start.17 = (f32[2,2,1,512]{3,2,0,1:T(1,128)}, f32[2,2,1,512]{3,2,0,1:T(1,128)}, u32[]{:S(2)}, u32[]{:S(2)}) collective-permute-start(f32[2,2,1,512]{3,2,0,1:T(1,128)} %slice.903), channel_id=1, source_target_pairs={{16,0},{32,16},{48,32},{64,48},{80,64},{96,80},{112,96},{17,1},{33... | collective-permute-start | bytes 24584 | tf_op jit(solution)/shard_map/ppermute | solution.py:18
  108.9 5.6 %collective-permute-start.16 = (f32[2,2,1024]{2,0,1:T(2,128)S(1)}, f32[2,2,1024]{2,0,1:T(2,128)S(1)}, u32[]{:S(2)}, u32[]{:S(2)}) collective-permute-start(f32[2,2,1024]{2,0,1:T(2,128)S(1)} %copy.120), channel_id=1, source_target_pairs={{1,0},{2,1},{3,2},{4,3},{5,4},{6,5},{7,6},{8,7},{9,8},{10,9},{11,1... | collective-permute-start | bytes 49160 | tf_op jit(solution)/shard_map/ppermute | solution.py:18
  118.4 11.4 %collective-permute-start.18 = (f32[2,2,1024]{2,0,1:T(2,128)S(1)}, f32[2,2,1024]{2,0,1:T(2,128)S(1)}, u32[]{:S(2)}, u32[]{:S(2)}) collective-permute-start(f32[2,2,1024]{2,0,1:T(2,128)S(1)} %copy.127), channel_id=1, source_target_pairs={{0,1},{1,2},{2,3},{3,4},{4,5},{5,6},{6,7},{7,8},{8,9},{9,10},{10,1... | collective-permute-start | bytes 49160 | tf_op jit(solution)/shard_map/ppermute | solution.py:18
  123.1 6.8 %collective-permute-start.19 = (f32[2,2,1,512]{3,2,1,0:T(1,128)S(1)}, f32[2,2,1,512]{3,2,1,0:T(1,128)S(1)}, u32[]{:S(2)}, u32[]{:S(2)}) collective-permute-start(f32[2,2,1,512]{3,2,1,0:T(1,128)S(1)} %slice.916), channel_id=1, source_target_pairs={{0,16},{16,32},{32,48},{48,64},{64,80},{80,96},{96,112},{1,17},{17... | collective-permute-start | bytes 24584 | tf_op jit(solution)/shard_map/ppermute | solution.py:18
  132.3 18.1 %copy-start.22 = (pred[16]{0:T(512)(128)(4,1)S(1)}, pred[16]{0:T(512)(128)(4,1)}, u32[]{:S(2)}) copy-start(pred[16]{0:T(512)(128)(4,1)} %copy-done.21) | copy-start | bytes 52
  (22 other events, 48.1 us)
where the time goes:
time: 153 us; the launch traced here: 151 us
  starting transfers between devices  63.7 us (42%)
  waiting for transfers between devices  29.3 us (19%)
  local copies, waits for them, and re-layouts  21.2 us (14%)
  blocking collectives  18.1 us (12%)
  other arithmetic  17.2 us (11%)
  between operations  1.69 us (1%)
    ppermute x20, starting transfers between devices, shifted_2(): lax.ppermute(value, axis, [(source, source + steps) for source in range(i...  63.7 us
    ppermute x20, waiting for transfers between devices, shifted_2(): lax.ppermute(value, axis, [(source, source + steps) for source in range(i...  29.3 us
    psum x1, blocking collectives, on_device(): collected = lax.psum(partial_value, 'wave')  18.1 us
    unnamed x55, local copies, waits for them, and re-layouts  8.55 us
    add x1, other arithmetic, coefficients(): decay_map = decay_map + chosen * decay[material_id]  5.68 us
  transfers between devices with their start and end apart: 20, of which 12 were waited for; matrix products, arithmetic and copies ran while one was open for 14% of the time, Pallas kernels for 0%

commit v1 on v0

v1 whole, which is shorter than its diff:
```python
import functools

import jax
import jax.numpy as jnp
from jax import lax
from jax.experimental import pallas as pl
from jax.experimental.pallas import tpu as pltpu
from jax.sharding import PartitionSpec as P

NZ = 64
STEPS = 5
NMAT = 3
LANES = 128
MESH = pl.DeviceIdType.MESH

time_step = 0.5
contrast = 2.0


def kernel(
    sizes,
    fields,
    profiles,
    waveforms,
    material_map,
    density,
    table,
    planes,
    box,
    grad_out,
    final_out,
    state,
    profile,
    source,
    coefs,
    inside,
    moves,
    duals,
    send_xe,
    send_xh,
    send_ye,
    send_yh,
    send_de,
    send_dh,
    recv_xe,
    recv_xh,
    recv_ye,
    recv_yh,
    recv_de,
    recv_dh,
    partial,
    core_in,
    half_sum,
    chip_in,
    total,
    send_sem,
    recv_sem,
    wave_send_sem,
    wave_recv_sem,
    load_sem,
    store_sem,
):
    n_wave, n_tx, n_ty, rows, flat = sizes
    chunks = flat // LANES
    wave = lax.axis_index("wave")
    tx = lax.axis_index("tx")
    ty = lax.axis_index("ty")
    tx_next, tx_prev = lax.rem(tx + 1, n_tx), lax.rem(tx + n_tx - 1, n_tx)
    ty_next, ty_prev = lax.rem(ty + 1, n_ty), lax.rem(ty + n_ty - 1, n_ty)
    core = lax.rem(wave, 2)
    wave_core = wave + 1 - 2 * core
    wave_chip = lax.rem(wave + 2, n_wave)

    load = pltpu.make_async_copy(fields.at[0], state, load_sem.at[0])
    load.start()
    load_profile = pltpu.make_async_copy(
        profiles.at[0, :, :, pl.ds(pl.multiple_of(ty * flat, LANES), flat)], profile, load_sem.at[1]
    )
    load_profile.start()

    barrier = pltpu.get_barrier_semaphore()
    partners = (
        {"tx": tx_prev},
        {"tx": tx_next},
        {"ty": ty_prev},
        {"ty": ty_next},
        {"tx": tx_prev, "ty": ty_next},
        {"tx": tx_next, "ty": ty_prev},
        {"wave": wave_core},
        {"wave": wave_chip},
    )
    for partner in partners:
        pl.semaphore_signal(barrier, inc=1, device_id=partner, device_id_type=MESH)

    row_id = lax.broadcasted_iota(jnp.int32, (rows, LANES), 0)
    lane_id = lax.broadcasted_iota(jnp.int32, (rows, LANES), 1)
    low = lane_id < NZ
    depth = lax.rem(lane_id, NZ)
    depth_first = depth == 0
    depth_last = depth == NZ - 1
    first_row = row_id == 0
    last_row = row_id == rows - 1

    def part(k):
        return slice(k * LANES, (k + 1) * LANES)

    def per_material(material, values):
        out = jnp.where(material == 0, values[0], values[1])
        for m in range(2, NMAT):
            out = jnp.where(material == m, values[m], out)
        return out

    for k in range(chunks):
        material = material_map[:, part(k)]
        eps = per_material(material, [table[m, 0] for m in range(NMAT)])
        spread = per_material(material, [table[m, 1] for m in range(NMAT)])
        omega = per_material(material, [table[m, 2] for m in range(NMAT)])
        damping = per_material(material, [table[m, 3] for m in range(NMAT)])
        x_id = row_id + tx * rows
        y_id = ty * (flat // NZ) + 2 * k + lane_id // NZ
        in_box = (
            (x_id >= box[0])
            & (x_id < box[1])
            & (y_id >= box[2])
            & (y_id < box[3])
            & (depth >= box[4])
            & (depth < box[5])
        )
        within = jnp.where(in_box, 1.0, 0.0)
        inside[:, part(k)] = within
        denom = 1.0 + 0.25 * damping
        drive = omega * omega * time_step / denom
        coefs[0, :, part(k)] = time_step / (eps + (within * density[:, part(k)]) * contrast)
        coefs[1, :, part(k)] = (1.0 - 0.25 * damping) / denom
        coefs[2, :, part(k)] = drive
        coefs[3, :, part(k)] = drive * spread

    load_profile.wait()
    for r in range(2):
        on_plane = jnp.where(row_id + tx * rows == planes[r], 1.0, 0.0)
        for c in range(3):
            for k in range(chunks):
                source[r, c, :, part(k)] = coefs[0, :, part(k)] * on_plane * profile[r, c : c + 1, part(k)]

    keep_x_next = jnp.where(tx == n_tx - 1, 0.0, 1.0)
    keep_x_prev = jnp.where(tx == 0, 0.0, 1.0)
    keep_y_next = jnp.where(ty == n_ty - 1, 0.0, 1.0)
    keep_y_prev = jnp.where(ty == 0, 0.0, 1.0)

    def roll(v, shift, axis):
        return pltpu.roll(v, shift % v.shape[axis], axis)

    def z_up(v):
        return jnp.where(depth_last, 0.0, roll(v, -1, 1))

    def z_down(v):
        return jnp.where(depth_first, 0.0, roll(v, 1, 1))

    def x_up(v):
        return jnp.where(last_row, 0.0, roll(v, -1, 0))

    def x_down(v, ghost):
        return jnp.where(first_row, ghost, roll(v, 1, 0))

    def y_up(vs):
        turned = [roll(v, NZ, 1) for v in vs]
        turned.append(jnp.zeros_like(turned[0]))
        return [jnp.where(low, turned[k], turned[k + 1]) for k in range(chunks)]

    def y_down(vs, ghost):
        turned = [ghost] + [roll(v, NZ, 1) for v in vs]
        return [jnp.where(low, turned[k], turned[k + 1]) for k in range(chunks)]

    def get(r, c):
        return [state[r, c, :, part(k)] for k in range(chunks)]

    def put(r, c, vs):
        for k in range(chunks):
            state[r, c, :, part(k)] = vs[k]

    load.wait()
    pl.semaphore_wait(barrier, len(partners))

    def step(n, carry):
        for r in range(2):
            ex, ey, ez = get(r, 0), get(r, 1), get(r, 2)
            y_ez, y_ex = y_up(ez), y_up(ex)
            for k in range(chunks):
                x_ez, x_ey = x_up(ez[k]), x_up(ey[k])
                z_ey, z_ex = z_up(ey[k]), z_up(ex[k])
                curl_x = (y_ez[k] - ez[k]) - (z_ey - ey[k])
                curl_y = (z_ex - ex[k]) - (x_ez - ez[k])
                curl_z = (x_ey - ey[k]) - (y_ex[k] - ex[k])
                hx = state[r, 3, :, part(k)] - time_step * curl_x
                hy = state[r, 4, :, part(k)] - time_step * curl_y
                hz = state[r, 5, :, part(k)] - time_step * curl_z
                state[r, 3, :, part(k)] = hx
                state[r, 4, :, part(k)] = hy
                state[r, 5, :, part(k)] = hz
                send_xe[n, 2 * r : 2 * r + 1, part(k)] = ey[k][0:1]
                send_xe[n, 2 * r + 1 : 2 * r + 2, part(k)] = ez[k][0:1]
                send_xh[n, 2 * r : 2 * r + 1, part(k)] = hy[rows - 1 : rows]
                send_xh[n, 2 * r + 1 : 2 * r + 2, part(k)] = hz[rows - 1 : rows]
                if k == 0:
                    send_ye[n, r] = jnp.where(low, ex[k], roll(ez[k], NZ, 1))
                    send_dh[n, r : r + 1] = ex[k][rows - 1 : rows]
                if k == chunks - 1:
                    send_yh[n, r] = jnp.where(low, roll(hx, NZ, 1), hz)
                    send_de[n, r : r + 1] = ey[k][0:1]

        copies = []
        flows = (
            (send_ye, recv_ye, {"ty": ty_prev}),
            (send_yh, recv_yh, {"ty": ty_next}),
            (send_de, recv_de, {"tx": tx_prev, "ty": ty_next}),
            (send_dh, recv_dh, {"tx": tx_next, "ty": ty_prev}),
            (send_xe, recv_xe, {"tx": tx_prev}),
            (send_xh, recv_xh, {"tx": tx_next}),
        )
        for i, (src, dst, target) in enumerate(flows):
            copy = pltpu.make_async_remote_copy(
                src_ref=src.at[n],
                dst_ref=dst.at[n],
                send_sem=send_sem.at[n, i],
                recv_sem=recv_sem.at[n, i],
                device_id=target,
                device_id_type=MESH,
            )
            copy.start()
            copies.append(copy)

        for r in range(2):
            for c in range(3):
                for k in range(chunks):
                    e = state[r, c, :, part(k)]
                    p = state[r, 6 + c, :, part(k)]
                    j = state[r, 9 + c, :, part(k)]
                    j = coefs[1, :, part(k)] * j + coefs[3, :, part(k)] * e - coefs[2, :, part(k)] * p
                    state[r, 9 + c, :, part(k)] = j
                    state[r, 6 + c, :, part(k)] = p + time_step * j

        for copy in copies:
            copy.wait_recv()

        for r in range(2):
            ex0, ez0 = state[r, 0, :, part(0)], state[r, 2, :, part(0)]
            got = recv_yh[n, r]
            corner = roll(jnp.broadcast_to(recv_de[n, r : r + 1], (rows, LANES)), NZ, 1) * keep_x_next
            line_hx = (got - time_step * ez0) * keep_y_prev
            line_hz = (
                roll(got, NZ, 1) + time_step * ex0 - jnp.where(last_row, time_step * corner, 0.0)
            ) * keep_y_prev
            row_hy, row_hz = [], []
            for k in range(chunks):
                hy = recv_xh[n, 2 * r : 2 * r + 1, part(k)] + time_step * state[r, 2, 0:1, part(k)]
                hz = recv_xh[n, 2 * r + 1 : 2 * r + 2, part(k)] - time_step * state[r, 1, 0:1, part(k)]
                if k == chunks - 1:
                    edge = roll(recv_dh[n, r : r + 1], NZ, 1) * keep_y_next
                    hz = hz + jnp.where(low[0:1], 0.0, time_step * edge)
                row_hy.append(hy * keep_x_prev)
                row_hz.append(hz * keep_x_prev)

            ahead = recv_ye[n, r] * (time_step * keep_y_next)
            k = chunks - 1
            state[r, 3, :, part(k)] = state[r, 3, :, part(k)] - jnp.where(low, 0.0, ahead)
            state[r, 5, :, part(k)] = state[r, 5, :, part(k)] + jnp.where(low, 0.0, roll(ahead, NZ, 1))
            for k in range(chunks):
                last = slice(rows - 1, rows)
                ey_next = recv_xe[n, 2 * r : 2 * r + 1, part(k)] * (time_step * keep_x_next)
                ez_next = recv_xe[n, 2 * r + 1 : 2 * r + 2, part(k)] * (time_step * keep_x_next)
                state[r, 4, last, part(k)] = state[r, 4, last, part(k)] + ez_next
                state[r, 5, last, part(k)] = state[r, 5, last, part(k)] - ey_next

            hx, hy, hz = get(r, 3), get(r, 4), get(r, 5)
            y_hz, y_hx = y_down(hz, line_hz), y_down(hx, line_hx)
            amount = waveforms[0, r, n]
            for k in range(chunks):
                x_hz, x_hy = x_down(hz[k], row_hz[k]), x_down(hy[k], row_hy[k])
                z_hy, z_hx = z_down(hy[k]), z_down(hx[k])
                curls = (
                    (hz[k] - y_hz[k]) - (hy[k] - z_hy),
                    (hx[k] - z_hx) - (hz[k] - x_hz),
                    (hy[k] - x_hy) - (hx[k] - y_hx[k]),
                )
                for c in range(3):
                    old = state[r, c, :, part(k)]
                    new = (
                        old
                        + coefs[0, :, part(k)] * (curls[c] - state[r, 9 + c, :, part(k)])
                        - amount * source[r, c, :, part(k)]
                    )
                    state[r, c, :, part(k)] = new
                    if r == 0:
                        moves[n, c, :, part(k)] = new - old
                    else:
                        duals[n, c, :, part(k)] = new
        return carry

    lax.fori_loop(0, STEPS, step, 0)

    store = pltpu.make_async_copy(state.at[:, 0:3], final_out.at[0], store_sem.at[0])
    store.start()

    for k in range(chunks):
        value = jnp.zeros((rows, LANES), jnp.float32)
        for n in range(STEPS):
            for c in range(3):
                value = value + duals[STEPS - 1 - n, c, :, part(k)] * moves[n, c, :, part(k)]
        partial[:, part(k)] = value

    half = rows // 2
    mine = pl.ds(pl.multiple_of(core * half, half), half)
    other = pl.ds(pl.multiple_of((1 - core) * half, half), half)

    def wave_copy(i, src, dst, target):
        return pltpu.make_async_remote_copy(
            src_ref=src,
            dst_ref=dst,
            send_sem=wave_send_sem.at[i],
            recv_sem=wave_recv_sem.at[i],
            device_id={"wave": target},
            device_id_type=MESH,
        )

    swap = wave_copy(0, partial.at[other], core_in, wave_core)
    swap.start()
    swap.wait_recv()
    half_sum[...] = partial[mine, :] + core_in[...]
    cross = wave_copy(1, half_sum, chip_in, wave_chip)
    cross.start()
    cross.wait_recv()
    total[mine, :] = (contrast * inside[mine, :]) * (half_sum[...] + chip_in[...])
    back = wave_copy(2, total.at[mine], total.at[mine], wave_core)
    back.start()
    back.wait_recv()
    grad = pltpu.make_async_copy(total, grad_out, store_sem.at[1])
    grad.start()

    swap.wait_send()
    cross.wait_send()
    back.wait_send()

    def drain(n, carry):
        for i, (src, dst, target) in enumerate(
            (
                (send_ye, recv_ye, {"ty": ty_prev}),
                (send_yh, recv_yh, {"ty": ty_next}),
                (send_de, recv_de, {"tx": tx_prev, "ty": ty_next}),
                (send_dh, recv_dh, {"tx": tx_next, "ty": ty_prev}),
                (send_xe, recv_xe, {"tx": tx_prev}),
                (send_xh, recv_xh, {"tx": tx_next}),
            )
        ):
            pltpu.make_async_remote_copy(
                src_ref=src.at[n],
                dst_ref=dst.at[n],
                send_sem=send_sem.at[n, i],
                recv_sem=recv_sem.at[n, i],
                device_id=target,
                device_id_type=MESH,
            ).wait_send()
        return carry

    lax.fori_loop(0, STEPS, drain, 0)
    store.wait()
    grad.wait()


def solution(mesh):
    n_wave, n_tx, n_ty = mesh.shape["wave"], mesh.shape["tx"], mesh.shape["ty"]

    def on_device(fields, profiles, waveforms, material_map, density, table, planes, box):
        rows, flat = material_map.shape
        f32 = jnp.float32
        vmem, smem, anywhere = pltpu.VMEM, pltpu.SMEM, pl.ANY
        spaces = (anywhere, anywhere, smem, vmem, vmem, smem, smem, smem)
        y_halo = (STEPS, 2, rows, LANES)
        x_halo = (STEPS, 4, flat)
        corner = (STEPS, 2, LANES)
        return pl.pallas_call(
            functools.partial(kernel, (n_wave, n_tx, n_ty, rows, flat)),
            out_shape=(
                jax.ShapeDtypeStruct((rows, flat), f32),
                jax.ShapeDtypeStruct((1, 2, 3, rows, flat), f32),
            ),
            in_specs=[pl.BlockSpec(memory_space=space) for space in spaces],
            out_specs=(pl.BlockSpec(memory_space=anywhere),) * 2,
            scratch_shapes=[
                vmem((2, 12, rows, flat), f32),
                vmem((2, 3, flat), f32),
                vmem((2, 3, rows, flat), f32),
                vmem((4, rows, flat), f32),
                vmem((rows, flat), f32),
                vmem((STEPS, 3, rows, flat), f32),
                vmem((STEPS, 3, rows, flat), f32),
                vmem(x_halo, f32),
                vmem(x_halo, f32),
                vmem(y_halo, f32),
                vmem(y_halo, f32),
                vmem(corner, f32),
                vmem(corner, f32),
                vmem(x_halo, f32),
                vmem(x_halo, f32),
                vmem(y_halo, f32),
                vmem(y_halo, f32),
                vmem(corner, f32),
                vmem(corner, f32),
                vmem((rows, flat), f32),
                vmem((rows // 2, flat), f32),
                vmem((rows // 2, flat), f32),
                vmem((rows // 2, flat), f32),
                vmem((rows, flat), f32),
                pltpu.SemaphoreType.DMA((STEPS, 6)),
                pltpu.SemaphoreType.DMA((STEPS, 6)),
                pltpu.SemaphoreType.DMA((3,)),
                pltpu.SemaphoreType.DMA((3,)),
                pltpu.SemaphoreType.DMA((2,)),
                pltpu.SemaphoreType.DMA((2,)),
            ],
            compiler_params=pltpu.CompilerParams(collective_id=0, has_side_effects=True),
        )(fields, profiles, waveforms, material_map, density, table, planes, box)

    placed = (
        P("wave", None, None, "tx", "ty"),
        P("wave", None, None, None),
        P("wave", None, None),
        P("tx", "ty"),
        P("tx", "ty"),
        P(),
        P(),
        P(),
    )
    return jax.shard_map(
        on_device,
        mesh=mesh,
        in_specs=placed,
        out_specs=(P("tx", "ty"), P("wave", None, None, "tx", "ty")),
        check_vma=False,
    )
```

time: 153 us -> 60 us (0.39)
  the two profiles are of different devices: /device:TPU:272 before, /device:TPU:1 now
where the time goes in v1:
time: 60 us; the launch traced here: 59.7 us
  Pallas kernels  54.3 us (90%)
  local copies, waits for them, and re-layouts  4.75 us (8%)
  between operations  0.64 us (1%)
    pallas_call x1, Pallas kernels, on_device(): pl.pallas_call(functools.partial(kernel, (n_wave, n_tx, n_ty, rows, flat)...  54.3 us
    unnamed x3, local copies, waits for them, and re-layouts  4.75 us

profile of v1, /device:TPU:1, one launch (start us, length us, event | category | flops | bytes accessed | tf_op | source)
XLA Modules:
  0.0 59.7 jit_solution(10675189217472886250)
XLA Ops:
  0.6 1.8 %copy.10.profiles = f32[1,2,3,8192]{3,2,1,0:T(4,128)} copy(f32[1,2,3,8192]{3,1,2,0:T(2,128)} %param.9) | data formatting | bytes 393216 | tf_op args[1]
  2.4 54.3 %shard_map.95 = (f32[16,512]{1,0:T(8,128)}, f32[1,2,3,16,512]{4,3,2,1,0:T(8,128)}) custom-call(f32[1,2,12,16,512]{4,3,2,1,0:T(8,128)} %fields.1, f32[1,2,3,8192]{3,2,1,0:T(4,128)} %copy.10.profiles, f32[1,2,5]{2,1,0:T(2,128)} %waveforms.1, s32[16,512]{1,0:T(8,128)} %material_map.1, f32[16,512]{1,0:T(8,128)} %density.1, f32[3,4]{1,0:T(4,128)} %table.1, ...), custom_call_target="tpu_custom_call" | custom-call | tf_op jit(solution)/shard_map/pallas_call | solution.py:380
  56.7 1.4 %copy.13 = f32[16,512]{1,0:T(8,128)} copy(f32[16,512]{1,0:T(8,128)} %get-tuple-element.4) | data formatting | bytes 65536
  58.1 1.6 %copy.14 = f32[1,2,3,16,512]{4,3,2,1,0:T(8,128)} copy(f32[1,2,3,16,512]{4,3,2,1,0:T(8,128)} %get-tuple-element.5) | data formatting | bytes 393216

commit v2 on v1

v2 whole, which is shorter than its diff:
```python
import functools

import jax
import jax.numpy as jnp
from jax import lax
from jax.experimental import pallas as pl
from jax.experimental.pallas import tpu as pltpu
from jax.sharding import PartitionSpec as P

NZ = 64
STEPS = 5
NMAT = 3
LANES = 128
REACH = 4
FLOWS = 16
MESH = pl.DeviceIdType.MESH

time_step = 0.5
contrast = 2.0


def kernel(
    sizes,
    fields,
    profiles,
    waveforms,
    material_map,
    density,
    table,
    planes,
    box,
    grad_out,
    final_out,
    alone,
    wide,
    profile,
    source,
    medium,
    coefs,
    inside,
    moves,
    duals,
    send_y,
    send_x,
    recv_ye,
    recv_yh,
    recv_yc,
    recv_x,
    recv_xc,
    far_x,
    far_y,
    partial,
    core_in,
    half_sum,
    chip_in,
    total,
    send_sem,
    recv_sem,
    once_send_sem,
    once_recv_sem,
    wave_send_sem,
    wave_recv_sem,
    load_sem,
    store_sem,
):
    n_wave, n_tx, n_ty, rows, flat = sizes
    chunks = flat // LANES
    wide_chunks = 2 * chunks
    wide_rows = rows + 2 * REACH
    edge = REACH * NZ
    wave = lax.axis_index("wave")
    tx = lax.axis_index("tx")
    ty = lax.axis_index("ty")
    tx_next, tx_prev = lax.rem(tx + 1, n_tx), lax.rem(tx + n_tx - 1, n_tx)
    ty_next, ty_prev = lax.rem(ty + 1, n_ty), lax.rem(ty + n_ty - 1, n_ty)
    core = lax.rem(wave, 2)
    wave_core = wave + 1 - 2 * core
    wave_chip = lax.rem(wave + 2, n_wave)

    load = pltpu.make_async_copy(fields.at[0], alone, load_sem.at[0])
    load.start()
    load_profile = pltpu.make_async_copy(
        profiles.at[0, :, :, pl.ds(pl.multiple_of(ty * flat, LANES), flat)], profile, load_sem.at[1]
    )
    load_profile.start()
    load_wide = pltpu.make_async_copy(fields.at[0], wide.at[:, :, 0:rows, 0:flat], load_sem.at[2])
    load_wide.start()

    barrier = pltpu.get_barrier_semaphore()
    low_low = {"tx": tx_prev, "ty": ty_prev}
    low_high = {"tx": tx_prev, "ty": ty_next}
    high_low = {"tx": tx_next, "ty": ty_prev}
    high_high = {"tx": tx_next, "ty": ty_next}
    partners = (
        {"ty": ty_prev},
        {"ty": ty_next},
        low_low,
        low_high,
        high_low,
        high_high,
        {"tx": tx_prev},
        {"tx": tx_next},
        {"wave": wave_chip},
        {"wave": wave_core},
    )
    for partner in partners:
        pl.semaphore_signal(barrier, inc=1, device_id=partner, device_id_type=MESH)

    def ids(count):
        row = lax.broadcasted_iota(jnp.int32, (count, LANES), 0)
        lane = lax.broadcasted_iota(jnp.int32, (count, LANES), 1)
        return row, lane, lane < NZ, lax.rem(lane, NZ)

    def part(k):
        return slice(k * LANES, (k + 1) * LANES)

    def per_material(material, values):
        out = jnp.where(material == 0, values[0], values[1])
        for m in range(2, NMAT):
            out = jnp.where(material == m, values[m], out)
        return out

    row_id, lane_id, low, depth = ids(rows)
    for k in range(chunks):
        material = material_map[:, part(k)]
        eps = per_material(material, [table[m, 0] for m in range(NMAT)])
        x_id = row_id + tx * rows
        y_id = ty * (flat // NZ) + 2 * k + lane_id // NZ
        in_box = (
            (x_id >= box[0])
            & (x_id < box[1])
            & (y_id >= box[2])
            & (y_id < box[3])
            & (depth >= box[4])
            & (depth < box[5])
        )
        within = jnp.where(in_box, 1.0, 0.0)
        inside[:, part(k)] = within
        medium[0, 0:rows, part(k)] = time_step / (eps + (within * density[:, part(k)]) * contrast)
        medium[1, 0:rows, part(k)] = material.astype(jnp.float32)

    def coefficients(reach, material):
        omega = per_material(material, [table[m, 2] for m in range(NMAT)])
        spread = per_material(material, [table[m, 1] for m in range(NMAT)])
        damping = per_material(material, [table[m, 3] for m in range(NMAT)])
        denom = 1.0 + 0.25 * damping
        drive = omega * omega * time_step / denom
        return reach, (1.0 - 0.25 * damping) / denom, drive, drive * spread

    for k in range(chunks):
        made = coefficients(medium[0, 0:rows, part(k)], material_map[:, part(k)])
        for i in range(4):
            coefs[i, 0:rows, part(k)] = made[i]

    load_profile.wait()
    for r in range(2):
        on_plane = jnp.where(row_id + tx * rows == planes[r], 1.0, 0.0)
        for c in range(3):
            for k in range(chunks):
                source[r, c, 0:rows, part(k)] = (
                    coefs[0, 0:rows, part(k)] * on_plane * profile[c, r : r + 1, part(k)]
                )
                source[r, c, rows:wide_rows, part(k)] = jnp.zeros((2 * REACH, LANES), jnp.float32)

    keep_x_next = jnp.where(tx == n_tx - 1, 0.0, 1.0)
    keep_x_prev = jnp.where(tx == 0, 0.0, 1.0)
    keep_y_next = jnp.where(ty == n_ty - 1, 0.0, 1.0)
    keep_y_prev = jnp.where(ty == 0, 0.0, 1.0)

    def roll(v, shift, axis):
        return pltpu.roll(v, shift % v.shape[axis], axis)

    def remote(src, dst, sems, target):
        return pltpu.make_async_remote_copy(
            src_ref=src,
            dst_ref=dst,
            send_sem=sems[0],
            recv_sem=sems[1],
            device_id=target,
            device_id_type=MESH,
        )

    top, bottom = slice(0, REACH), slice(rows - REACH, rows)
    after, before = slice(rows, rows + REACH), slice(rows + REACH, wide_rows)
    left, right = slice(0, edge), slice(flat - edge, flat)
    beyond, ahead_of = slice(flat, flat + edge), slice(flat + edge, flat + 2 * edge)
    whole, inner = slice(0, rows), slice(0, flat)

    def medium_copies():
        ways = (
            ({"ty": ty_prev}, whole, left, whole, beyond),
            ({"ty": ty_next}, whole, right, whole, ahead_of),
            (low_low, top, left, after, beyond),
            (low_high, top, right, after, ahead_of),
            (high_low, bottom, left, before, beyond),
            (high_high, bottom, right, before, ahead_of),
            ({"tx": tx_prev}, top, inner, after, inner),
            ({"tx": tx_next}, bottom, inner, before, inner),
        )
        return [
            remote(
                medium.at[:, a, b],
                medium.at[:, c, d],
                (once_send_sem.at[i], once_recv_sem.at[i]),
                target,
            )
            for i, (target, a, b, c, d) in enumerate(ways)
        ]

    def far_copies():
        return [
            remote(
                send_x.at[0, 0:4, LANES : 2 * LANES],
                far_x.at[0:4],
                (once_send_sem.at[8], once_recv_sem.at[8]),
                low_high,
            ),
            remote(
                send_y.at[0, :, rows - 2 * REACH : rows - REACH, 0:LANES],
                far_y.at[:, 0:REACH],
                (once_send_sem.at[9], once_recv_sem.at[9]),
                high_low,
            ),
        ]

    def trace_copies(n):
        e_part, h_part = slice(0, LANES), slice(LANES, 2 * LANES)
        e_rows, h_rows = slice(0, 4), slice(4, 8)
        ways = (
            ({"ty": ty_prev}, send_y.at[n, :, :, e_part], recv_ye.at[n, :, whole]),
            ({"ty": ty_next}, send_y.at[n, :, :, h_part], recv_yh.at[n, :, whole]),
            (low_low, send_y.at[n, :, top, e_part], recv_ye.at[n, :, after]),
            (low_low, send_x.at[n, e_rows, left], recv_x.at[n, e_rows, beyond]),
            (low_high, send_y.at[n, :, top, h_part], recv_yh.at[n, :, after]),
            (low_high, send_x.at[n, e_rows, right], recv_x.at[n, e_rows, ahead_of]),
            (high_low, send_y.at[n, :, bottom, e_part], recv_ye.at[n, :, before]),
            (high_low, send_x.at[n, h_rows, left], recv_x.at[n, h_rows, beyond]),
            (high_high, send_y.at[n, :, bottom, h_part], recv_yh.at[n, :, before]),
            (high_high, send_x.at[n, h_rows, right], recv_x.at[n, h_rows, ahead_of]),
            ({"ty": ty_prev}, send_x.at[n, :, left], recv_xc.at[n, :, 0:edge]),
            ({"ty": ty_next}, send_x.at[n, :, right], recv_xc.at[n, :, edge : 2 * edge]),
            ({"tx": tx_prev}, send_x.at[n, e_rows, :], recv_x.at[n, e_rows, inner]),
            ({"tx": tx_next}, send_x.at[n, h_rows, :], recv_x.at[n, h_rows, inner]),
            ({"tx": tx_prev}, send_y.at[n, :, top, :], recv_yc.at[n, :, 0:REACH]),
            ({"tx": tx_next}, send_y.at[n, :, bottom, :], recv_yc.at[n, :, REACH : 2 * REACH]),
        )
        return [
            remote(src, dst, (send_sem.at[n, i], recv_sem.at[n, i]), target)
            for i, (target, src, dst) in enumerate(ways)
        ]

    load.wait()
    pl.semaphore_wait(barrier, len(partners))
    for copy in medium_copies():
        copy.start()

    def alone_step(n, carry):
        depth_first, depth_last = depth == 0, depth == NZ - 1
        first_row, last_row = row_id == 0, row_id == rows - 1

        def y_up(vs):
            turned = [roll(v, NZ, 1) for v in vs] + [jnp.zeros((rows, LANES), jnp.float32)]
            return [jnp.where(low, turned[k], turned[k + 1]) for k in range(chunks)]

        def y_down(vs):
            turned = [jnp.zeros((rows, LANES), jnp.float32)] + [roll(v, NZ, 1) for v in vs]
            return [jnp.where(low, turned[k], turned[k + 1]) for k in range(chunks)]

        def get(r, c):
            return [alone[r, c, :, part(k)] for k in range(chunks)]

        for r in range(2):
            ex, ey, ez = get(r, 0), get(r, 1), get(r, 2)
            y_ez, y_ex = y_up(ez), y_up(ex)
            for k in range(chunks):
                x_ez = jnp.where(last_row, 0.0, roll(ez[k], -1, 0))
                x_ey = jnp.where(last_row, 0.0, roll(ey[k], -1, 0))
                z_ey = jnp.where(depth_last, 0.0, roll(ey[k], -1, 1))
                z_ex = jnp.where(depth_last, 0.0, roll(ex[k], -1, 1))
                curl_x = (y_ez[k] - ez[k]) - (z_ey - ey[k])
                curl_y = (z_ex - ex[k]) - (x_ez - ez[k])
                curl_z = (x_ey - ey[k]) - (y_ex[k] - ex[k])
                hx = alone[r, 3, :, part(k)] - time_step * curl_x
                hy = alone[r, 4, :, part(k)] - time_step * curl_y
                hz = alone[r, 5, :, part(k)] - time_step * curl_z
                alone[r, 3, :, part(k)] = hx
                alone[r, 4, :, part(k)] = hy
                alone[r, 5, :, part(k)] = hz
                send_x[n, 2 * r : 2 * r + 1, part(k)] = ey[k][0:1]
                send_x[n, 2 * r + 1 : 2 * r + 2, part(k)] = ez[k][0:1]
                send_x[n, 4 + 2 * r : 5 + 2 * r, part(k)] = hy[rows - 1 : rows]
                send_x[n, 5 + 2 * r : 6 + 2 * r, part(k)] = hz[rows - 1 : rows]
                if k == 0:
                    send_y[n, r, :, 0:LANES] = jnp.where(low, ex[k], roll(ez[k], NZ, 1))
                if k == chunks - 1:
                    send_y[n, r, :, LANES : 2 * LANES] = jnp.where(low, roll(hx, NZ, 1), hz)

        for copy in trace_copies(n):
            copy.start()

        @pl.when(n == 0)
        def _():
            for copy in far_copies():
                copy.start()

        @pl.when(n < STEPS - 1)
        def _():
            for r in range(2):
                hx, hy, hz = get(r, 3), get(r, 4), get(r, 5)
                y_hz, y_hx = y_down(hz), y_down(hx)
                amount = waveforms[0, r, n]
                for k in range(chunks):
                    x_hz = jnp.where(first_row, 0.0, roll(hz[k], 1, 0))
                    x_hy = jnp.where(first_row, 0.0, roll(hy[k], 1, 0))
                    z_hy = jnp.where(depth_first, 0.0, roll(hy[k], 1, 1))
                    z_hx = jnp.where(depth_first, 0.0, roll(hx[k], 1, 1))
                    curls = (
                        (hz[k] - y_hz[k]) - (hy[k] - z_hy),
                        (hx[k] - z_hx) - (hz[k] - x_hz),
                        (hy[k] - x_hy) - (hx[k] - y_hx[k]),
                    )
                    for c in range(3):
                        e = alone[r, c, :, part(k)]
                        p = alone[r, 6 + c, :, part(k)]
                        j = alone[r, 9 + c, :, part(k)]
                        j = (
                            coefs[1, 0:rows, part(k)] * j
                            + coefs[3, 0:rows, part(k)] * e
                            - coefs[2, 0:rows, part(k)] * p
                        )
                        alone[r, 9 + c, :, part(k)] = j
                        alone[r, 6 + c, :, part(k)] = p + time_step * j
                        alone[r, c, :, part(k)] = (
                            e
                            + coefs[0, 0:rows, part(k)] * (curls[c] - j)
                            - amount * source[r, c, 0:rows, part(k)]
                        )

        return carry

    lax.fori_loop(0, STEPS, alone_step, 0)

    load_wide.wait()
    for r in range(2):
        for c in range(12):
            for k in range(wide_chunks):
                if k < chunks:
                    wide[r, c, rows:wide_rows, part(k)] = jnp.zeros((2 * REACH, LANES), jnp.float32)
                else:
                    wide[r, c, :, part(k)] = jnp.zeros((wide_rows, LANES), jnp.float32)

    for copy in medium_copies():
        copy.wait_recv()
    row_id, lane_id, low, depth = ids(wide_rows)
    near_row = jnp.where(row_id < rows + REACH, row_id, row_id - wide_rows)
    x_in = (near_row + tx * rows >= 0) & (near_row + tx * rows < n_tx * rows)
    for k in range(wide_chunks):
        line = 2 * k if k < chunks + chunks // 2 else 2 * (k - wide_chunks)
        y_id = ty * (flat // NZ) + line + lane_id // NZ
        present = x_in & (y_id >= 0) & (y_id < n_ty * (flat // NZ))
        made = coefficients(medium[0, :, part(k)], medium[1, :, part(k)])
        coefs[0, :, part(k)] = jnp.where(present, made[0], 0.0)
        for i in range(1, 4):
            coefs[i, :, part(k)] = made[i]
        coefs[4, :, part(k)] = jnp.where(present, time_step, 0.0)

    for copy in far_copies():
        copy.wait_recv()

    def wide_step(n, carry):
        depth_first, depth_last = depth == 0, depth == NZ - 1
        start = jnp.where(n == 0, 1.0, 0.0)
        for copy in trace_copies(n):
            copy.wait_recv()

        def get(r, c):
            return [wide[r, c, :, part(k)] for k in range(wide_chunks)]

        def tall(v):
            return jnp.concatenate([jnp.zeros((rows, LANES), jnp.float32), v], axis=0)

        def at_row(i, v):
            return jnp.where(row_id == i, v, 0.0)

        def y_up(vs, inner_edge, outer_edge):
            turned = [roll(v, NZ, 1) for v in vs]
            out = []
            for k in range(wide_chunks):
                other = turned[(k + 1) % wide_chunks]
                if k == chunks - 1:
                    other = other + inner_edge
                if k == chunks + chunks // 2 - 1:
                    other = jnp.zeros_like(other)
                if k == wide_chunks - 1:
                    other = other + outer_edge
                out.append(jnp.where(low, turned[k], other))
            return out

        def y_down(vs, inner_edge, outer_edge, far):
            turned = [roll(v, NZ, 1) for v in vs]
            out = []
            for k in range(wide_chunks):
                other = turned[(k - 1) % wide_chunks]
                if k == 0:
                    other = other + inner_edge
                if k == chunks:
                    other = other + outer_edge
                if k == chunks + chunks // 2:
                    other = far
                out.append(jnp.where(low, other, turned[k]))
            return out

        zero = jnp.zeros((wide_rows, LANES), jnp.float32)
        for r in range(2):
            def x_up(v, k, c):
                out = roll(v, -1, 0) + at_row(rows - 1, keep_x_next * recv_x[n, 2 * r + c : 2 * r + c + 1, part(k)])
                if k >= chunks:
                    out = out + at_row(wide_rows - 1, recv_xc[n, 2 * r + c : 2 * r + c + 1, part(k - chunks)])
                return out

            def x_down(v, k, c, far):
                i = 4 + 2 * r + c
                out = jnp.where(row_id == rows + REACH, far, roll(v, 1, 0))
                out = out + at_row(0, keep_x_prev * recv_x[n, i : i + 1, part(k)])
                if k >= chunks:
                    out = out + at_row(rows, recv_xc[n, i : i + 1, part(k - chunks)])
                return out

            ex, ey, ez = get(r, 0), get(r, 1), get(r, 2)
            got = recv_ye[n, r] * keep_y_next
            corner = tall(recv_yc[n, r, :, 0:LANES])
            y_ez = y_up(ez, got, corner)
            y_ex = y_up(ex, roll(got, NZ, 1), roll(corner, NZ, 1))
            for k in range(wide_chunks):
                x_ez, x_ey = x_up(ez[k], k, 1), x_up(ey[k], k, 0)
                z_ey = jnp.where(depth_last, 0.0, roll(ey[k], -1, 1))
                z_ex = jnp.where(depth_last, 0.0, roll(ex[k], -1, 1))
                curls = (
                    (y_ez[k] - ez[k]) - (z_ey - ey[k]),
                    (z_ex - ex[k]) - (x_ez - ez[k]),
                    (x_ey - ey[k]) - (y_ex[k] - ex[k]),
                )
                for c in range(3):
                    wide[r, 3 + c, :, part(k)] = wide[r, 3 + c, :, part(k)] - coefs[4, :, part(k)] * curls[c]

            hx, hy, hz = get(r, 3), get(r, 4), get(r, 5)
            got = recv_yh[n, r] * keep_y_prev
            corner = tall(recv_yc[n, r, :, LANES : 2 * LANES])
            far_line = at_row(
                rows - 1, (-time_step * start * keep_x_next) * roll(far_x[2 * r : 2 * r + 1], NZ, 1)
            )
            far_row = jnp.where(
                low[0:1], 0.0, (time_step * start * keep_y_next) * roll(far_y[r, REACH - 1 : REACH], NZ, 1)
            )
            y_hx = y_down(hx, got, corner, zero)
            y_hz = y_down(hz, roll(got, NZ, 1), roll(corner, NZ, 1), far_line)
            amount = waveforms[0, r, n]
            for k in range(wide_chunks):
                x_hz = x_down(hz[k], k, 1, far_row if k == chunks - 1 else 0.0)
                x_hy = x_down(hy[k], k, 0, 0.0)
                z_hy = jnp.where(depth_first, 0.0, roll(hy[k], 1, 1))
                z_hx = jnp.where(depth_first, 0.0, roll(hx[k], 1, 1))
                curls = (
                    (hz[k] - y_hz[k]) - (hy[k] - z_hy),
                    (hx[k] - z_hx) - (hz[k] - x_hz),
                    (hy[k] - x_hy) - (hx[k] - y_hx[k]),
                )
                for c in range(3):
                    e = wide[r, c, :, part(k)]
                    p = wide[r, 6 + c, :, part(k)]
                    j = wide[r, 9 + c, :, part(k)]
                    j = coefs[1, :, part(k)] * j + coefs[3, :, part(k)] * e - coefs[2, :, part(k)] * p
                    wide[r, 9 + c, :, part(k)] = j
                    wide[r, 6 + c, :, part(k)] = p + time_step * j
                    new = e + coefs[0, :, part(k)] * (curls[c] - j)
                    if k < chunks:
                        new = new - amount * source[r, c, :, part(k)]
                        if r == 0:
                            moves[n, c, :, part(k)] = new[0:rows] - e[0:rows]
                        else:
                            duals[n, c, :, part(k)] = new[0:rows]
                    wide[r, c, :, part(k)] = new
        return carry

    lax.fori_loop(0, STEPS, wide_step, 0)

    store = pltpu.make_async_copy(wide.at[:, 0:3, 0:rows, 0:flat], final_out.at[0], store_sem.at[0])
    store.start()

    for k in range(chunks):
        value = jnp.zeros((rows, LANES), jnp.float32)
        for n in range(STEPS):
            for c in range(3):
                value = value + duals[STEPS - 1 - n, c, :, part(k)] * moves[n, c, :, part(k)]
        partial[:, part(k)] = value

    half = rows // 2
    mine = pl.ds(pl.multiple_of(core * half, half), half)
    other = pl.ds(pl.multiple_of((1 - core) * half, half), half)

    def wave_copy(i, src, dst, target):
        return pltpu.make_async_remote_copy(
            src_ref=src,
            dst_ref=dst,
            send_sem=wave_send_sem.at[i],
            recv_sem=wave_recv_sem.at[i],
            device_id={"wave": target},
            device_id_type=MESH,
        )

    swap = wave_copy(0, partial.at[other], core_in, wave_core)
    swap.start()
    swap.wait_recv()
    half_sum[...] = partial[mine, :] + core_in[...]
    cross = wave_copy(1, half_sum, chip_in, wave_chip)
    cross.start()
    cross.wait_recv()
    total[mine, :] = (contrast * inside[mine, :]) * (half_sum[...] + chip_in[...])
    back = wave_copy(2, total.at[mine], total.at[mine], wave_core)
    back.start()
    back.wait_recv()
    grad = pltpu.make_async_copy(total, grad_out, store_sem.at[1])
    grad.start()

    swap.wait_send()
    cross.wait_send()
    back.wait_send()

    for copy in medium_copies() + far_copies():
        copy.wait_send()

    def drain(n, carry):
        for copy in trace_copies(n):
            copy.wait_send()
        return carry

    lax.fori_loop(0, STEPS, drain, 0)
    store.wait()
    grad.wait()


def solution(mesh):
    n_wave, n_tx, n_ty = mesh.shape["wave"], mesh.shape["tx"], mesh.shape["ty"]

    def on_device(fields, profiles, waveforms, material_map, density, table, planes, box):
        rows, flat = material_map.shape
        f32 = jnp.float32
        vmem, smem, anywhere = pltpu.VMEM, pltpu.SMEM, pl.ANY
        spaces = (anywhere, anywhere, smem, vmem, vmem, smem, smem, smem)
        wide_rows, wide_flat = rows + 2 * REACH, flat + 2 * REACH * NZ
        return pl.pallas_call(
            functools.partial(kernel, (n_wave, n_tx, n_ty, rows, flat)),
            out_shape=(
                jax.ShapeDtypeStruct((rows, flat), f32),
                jax.ShapeDtypeStruct((1, 2, 3, rows, flat), f32),
            ),
            in_specs=[pl.BlockSpec(memory_space=space) for space in spaces],
            out_specs=(pl.BlockSpec(memory_space=anywhere),) * 2,
            scratch_shapes=[
                vmem((2, 12, rows, flat), f32),
                vmem((2, 12, wide_rows, wide_flat), f32),
                vmem((3, 2, flat), f32),
                vmem((2, 3, wide_rows, flat), f32),
                vmem((2, wide_rows, wide_flat), f32),
                vmem((5, wide_rows, wide_flat), f32),
                vmem((rows, flat), f32),
                vmem((STEPS, 3, rows, flat), f32),
                vmem((STEPS, 3, rows, flat), f32),
                vmem((STEPS, 2, rows, 2 * LANES), f32),
                vmem((STEPS, 8, flat), f32),
                vmem((STEPS, 2, wide_rows, LANES), f32),
                vmem((STEPS, 2, wide_rows, LANES), f32),
                vmem((STEPS, 2, 2 * REACH, 2 * LANES), f32),
                vmem((STEPS, 8, wide_flat), f32),
                vmem((STEPS, 8, 2 * REACH * NZ), f32),
                vmem((8, LANES), f32),
                vmem((2, 8, LANES), f32),
                vmem((rows, flat), f32),
                vmem((rows // 2, flat), f32),
                vmem((rows // 2, flat), f32),
                vmem((rows // 2, flat), f32),
                vmem((rows, flat), f32),
                pltpu.SemaphoreType.DMA((STEPS, FLOWS)),
                pltpu.SemaphoreType.DMA((STEPS, FLOWS)),
                pltpu.SemaphoreType.DMA((10,)),
                pltpu.SemaphoreType.DMA((10,)),
                pltpu.SemaphoreType.DMA((3,)),
                pltpu.SemaphoreType.DMA((3,)),
                pltpu.SemaphoreType.DMA((3,)),
                pltpu.SemaphoreType.DMA((2,)),
            ],
            compiler_params=pltpu.CompilerParams(collective_id=0, has_side_effects=True),
        )(fields, jnp.transpose(profiles, (0, 2, 1, 3)), waveforms, material_map, density, table, planes, box)

    placed = (
        P("wave", None, None, "tx", "ty"),
        P("wave", None, None, None),
        P("wave", None, None),
        P("tx", "ty"),
        P("tx", "ty"),
        P(),
        P(),
        P(),
    )
    return jax.shard_map(
        on_device,
        mesh=mesh,
        in_specs=placed,
        out_specs=(P("tx", "ty"), P("wave", None, None, "tx", "ty")),
        check_vma=False,
    )
```

time: 60 us -> 44.2 us (0.74)
  Pallas kernels: 54.3 us -> 40.3 us
  local copies, waits for them, and re-layouts: 4.75 us -> 2.99 us
    pallas_call x1, Pallas kernels: 54.3 us -> 40.3 us  [on_device(): pl.pallas_call(functools.partial(kernel, (n_wave, n_tx, n_ty, rows, flat)...]
    unnamed x3 -> x2, local copies, waits for them, and re-layouts: 4.75 us -> 2.99 us
where the time goes in v2:
time: 44.2 us; the launch traced here: 43.9 us
  Pallas kernels  40.3 us (91%)
  local copies, waits for them, and re-layouts  2.99 us (7%)
  between operations  0.64 us (1%)
    pallas_call x1, Pallas kernels, on_device(): pl.pallas_call(functools.partial(kernel, (n_wave, n_tx, n_ty, rows, flat)...  40.3 us
    unnamed x2, local copies, waits for them, and re-layouts  2.99 us

profile of v2, /device:TPU:1, one launch (start us, length us, event | category | flops | bytes accessed | tf_op | source)
XLA Modules:
  0.0 43.9 jit_solution(9905645446495352074)
XLA Ops:
  0.6 40.3 %shard_map.95 = (f32[16,512]{1,0:T(8,128)}, f32[1,2,3,16,512]{4,3,2,1,0:T(8,128)}) custom-call(f32[1,2,12,16,512]{4,3,2,1,0:T(8,128)} %fields.1, f32[1,3,2,8192]{3,2,1,0:T(2,128)} %bitcast.1, f32[1,2,5]{2,1,0:T(2,128)} %waveforms.1, s32[16,512]{1,0:T(8,128)} %material_map.1, f32[16,512]{1,0:T(8,128)} %density.1, f32[3,4]{1,0:T(4,128)} %table.1, s32[2]{0:T(128)} %planes.1, ...), custom_call_target="tpu_custom_call" | custom-call | tf_op jit(solution)/shard_map/pallas_call | solution.py:551
  40.9 1.4 %copy.12 = f32[16,512]{1,0:T(8,128)} copy(f32[16,512]{1,0:T(8,128)} %get-tuple-element.4) | data formatting | bytes 65536
  42.3 1.6 %copy.13 = f32[1,2,3,16,512]{4,3,2,1,0:T(8,128)} copy(f32[1,2,3,16,512]{4,3,2,1,0:T(8,128)} %get-tuple-element.5) | data formatting | bytes 393216

commit v3 on v2

--- a/solution.py
+++ b/solution.py
@@ -12,7 +12,7 @@
 NMAT = 3
 LANES = 128
 REACH = 4
-FLOWS = 16
+FLOWS = 8
 MESH = pl.DeviceIdType.MESH
 
 time_step = 0.5
@@ -23,12 +23,12 @@
     sizes,
     fields,
     profiles,
-    waveforms,
-    material_map,
-    density,
-    table,
-    planes,
-    box,
+    waveforms_in,
+    material_in,
+    density_in,
+    table_in,
+    planes_in,
+    box_in,
     grad_out,
     final_out,
     alone,
@@ -40,20 +40,28 @@
     inside,
     moves,
     duals,
-    send_y,
-    send_x,
-    recv_ye,
-    recv_yh,
-    recv_yc,
-    recv_x,
-    recv_xc,
-    far_x,
-    far_y,
+    send_a,
+    send_b,
+    send_c,
+    send_d,
+    recv_a,
+    recv_b,
+    recv_c,
+    recv_d,
+    recv_ahead_up,
+    recv_ahead_down,
+    recv_back_up,
+    recv_back_down,
+    waveforms,
+    material_map,
+    density,
+    table,
+    planes,
+    box,
     partial,
     core_in,
     half_sum,
     chip_in,
-    total,
     send_sem,
     recv_sem,
     once_send_sem,
@@ -77,12 +85,29 @@
     wave_core = wave + 1 - 2 * core
     wave_chip = lax.rem(wave + 2, n_wave)
 
-    load = pltpu.make_async_copy(fields.at[0], alone, load_sem.at[0])
+    load = pltpu.make_async_copy(fields.at[0, :, 0:6], alone.at[:, 0:6], load_sem.at[0])
     load.start()
+    load_rest = pltpu.make_async_copy(fields.at[0, :, 6:12], alone.at[:, 6:12], load_sem.at[3])
+    load_rest.start()
     load_profile = pltpu.make_async_copy(
         profiles.at[0, :, :, pl.ds(pl.multiple_of(ty * flat, LANES), flat)], profile, load_sem.at[1]
     )
     load_profile.start()
+    small = [
+        pltpu.make_async_copy(src, dst, load_sem.at[4 + i])
+        for i, (src, dst) in enumerate(
+            (
+                (material_in, material_map),
+                (density_in, density),
+                (table_in, table),
+                (box_in, box),
+                (planes_in, planes),
+                (waveforms_in, waveforms),
+            )
+        )
+    ]
+    for copy in small:
+        copy.start()
     load_wide = pltpu.make_async_copy(fields.at[0], wide.at[:, :, 0:rows, 0:flat], load_sem.at[2])
     load_wide.start()
 
@@ -121,23 +146,6 @@
         return out
 
     row_id, lane_id, low, depth = ids(rows)
-    for k in range(chunks):
-        material = material_map[:, part(k)]
-        eps = per_material(material, [table[m, 0] for m in range(NMAT)])
-        x_id = row_id + tx * rows
-        y_id = ty * (flat // NZ) + 2 * k + lane_id // NZ
-        in_box = (
-            (x_id >= box[0])
-            & (x_id < box[1])
-            & (y_id >= box[2])
-            & (y_id < box[3])
-            & (depth >= box[4])
-            & (depth < box[5])
-        )
-        within = jnp.where(in_box, 1.0, 0.0)
-        inside[:, part(k)] = within
-        medium[0, 0:rows, part(k)] = time_step / (eps + (within * density[:, part(k)]) * contrast)
-        medium[1, 0:rows, part(k)] = material.astype(jnp.float32)
 
     def coefficients(reach, material):
         omega = per_material(material, [table[m, 2] for m in range(NMAT)])
@@ -147,20 +155,41 @@
         drive = omega * omega * time_step / denom
         return reach, (1.0 - 0.25 * damping) / denom, drive, drive * spread
 
-    for k in range(chunks):
-        made = coefficients(medium[0, 0:rows, part(k)], material_map[:, part(k)])
-        for i in range(4):
-            coefs[i, 0:rows, part(k)] = made[i]
-
-    load_profile.wait()
-    for r in range(2):
-        on_plane = jnp.where(row_id + tx * rows == planes[r], 1.0, 0.0)
-        for c in range(3):
-            for k in range(chunks):
-                source[r, c, 0:rows, part(k)] = (
-                    coefs[0, 0:rows, part(k)] * on_plane * profile[c, r : r + 1, part(k)]
-                )
-                source[r, c, rows:wide_rows, part(k)] = jnp.zeros((2 * REACH, LANES), jnp.float32)
+    def prepare():
+        for copy in small:
+            copy.wait()
+        load_rest.wait()
+        load_profile.wait()
+        for k in range(chunks):
+            material = material_map[:, part(k)]
+            eps = per_material(material, [table[m, 0] for m in range(NMAT)])
+            x_id = row_id + tx * rows
+            y_id = ty * (flat // NZ) + 2 * k + lane_id // NZ
+            in_box = (
+                (x_id >= box[0])
+                & (x_id < box[1])
+                & (y_id >= box[2])
+                & (y_id < box[3])
+                & (depth >= box[4])
+                & (depth < box[5])
+            )
+            within = jnp.where(in_box, 1.0, 0.0)
+            inside[:, part(k)] = within
+            medium[0, 0:rows, part(k)] = time_step / (eps + (within * density[:, part(k)]) * contrast)
+            medium[1, 0:rows, part(k)] = material.astype(jnp.float32)
+        for k in range(chunks):
+            made = coefficients(medium[0, 0:rows, part(k)], material_map[:, part(k)])
+            for i in range(4):
+                coefs[i, 0:rows, part(k)] = made[i]
+
+        for r in range(2):
+            on_plane = jnp.where(row_id + tx * rows == planes[r], 1.0, 0.0)
+            for c in range(3):
+                for k in range(chunks):
+                    source[r, c, 0:rows, part(k)] = (
+                        coefs[0, 0:rows, part(k)] * on_plane * profile[c, r : r + 1, part(k)]
+                    )
+                    source[r, c, rows:wide_rows, part(k)] = jnp.zeros((2 * REACH, LANES), jnp.float32)
 
     keep_x_next = jnp.where(tx == n_tx - 1, 0.0, 1.0)
     keep_x_prev = jnp.where(tx == 0, 0.0, 1.0)
@@ -199,60 +228,68 @@
         )
         return [
             remote(
-                medium.at[:, a, b],
-                medium.at[:, c, d],
+                medium.at[core, a, b],
+                medium.at[core, c, d],
                 (once_send_sem.at[i], once_recv_sem.at[i]),
                 target,
             )
             for i, (target, a, b, c, d) in enumerate(ways)
         ]
 
-    def far_copies():
+    def shared_copies(plane):
+        areas = ((slice(0, rows), slice(flat, 2 * flat)), (slice(rows, wide_rows), slice(0, 2 * flat)))
         return [
             remote(
-                send_x.at[0, 0:4, LANES : 2 * LANES],
-                far_x.at[0:4],
-                (once_send_sem.at[8], once_recv_sem.at[8]),
-                low_high,
-            ),
-            remote(
-                send_y.at[0, :, rows - 2 * REACH : rows - REACH, 0:LANES],
-                far_y.at[:, 0:REACH],
-                (once_send_sem.at[9], once_recv_sem.at[9]),
-                high_low,
-            ),
+                medium.at[plane, a, b],
+                medium.at[plane, a, b],
+                (once_send_sem.at[8 + i], once_recv_sem.at[8 + i]),
+                {"wave": wave_core},
+            )
+            for i, (a, b) in enumerate(areas)
         ]
 
     def trace_copies(n):
-        e_part, h_part = slice(0, LANES), slice(LANES, 2 * LANES)
-        e_rows, h_rows = slice(0, 4), slice(4, 8)
+        always, first, later = None, n == 0, n > 0
+        early, late, before_last = n < 2, n >= 2, n < STEPS - 1
         ways = (
-            ({"ty": ty_prev}, send_y.at[n, :, :, e_part], recv_ye.at[n, :, whole]),
-            ({"ty": ty_next}, send_y.at[n, :, :, h_part], recv_yh.at[n, :, whole]),
-            (low_low, send_y.at[n, :, top, e_part], recv_ye.at[n, :, after]),
-            (low_low, send_x.at[n, e_rows, left], recv_x.at[n, e_rows, beyond]),
-            (low_high, send_y.at[n, :, top, h_part], recv_yh.at[n, :, after]),
-            (low_high, send_x.at[n, e_rows, right], recv_x.at[n, e_rows, ahead_of]),
-            (high_low, send_y.at[n, :, bottom, e_part], recv_ye.at[n, :, before]),
-            (high_low, send_x.at[n, h_rows, left], recv_x.at[n, h_rows, beyond]),
-            (high_high, send_y.at[n, :, bottom, h_part], recv_yh.at[n, :, before]),
-            (high_high, send_x.at[n, h_rows, right], recv_x.at[n, h_rows, ahead_of]),
-            ({"ty": ty_prev}, send_x.at[n, :, left], recv_xc.at[n, :, 0:edge]),
-            ({"ty": ty_next}, send_x.at[n, :, right], recv_xc.at[n, :, edge : 2 * edge]),
-            ({"tx": tx_prev}, send_x.at[n, e_rows, :], recv_x.at[n, e_rows, inner]),
-            ({"tx": tx_next}, send_x.at[n, h_rows, :], recv_x.at[n, h_rows, inner]),
-            ({"tx": tx_prev}, send_y.at[n, :, top, :], recv_yc.at[n, :, 0:REACH]),
-            ({"tx": tx_next}, send_y.at[n, :, bottom, :], recv_yc.at[n, :, REACH : 2 * REACH]),
+            (early, 0, {"ty": ty_prev}, send_c.at[n, 0:6], recv_c.at[n, 0:6]),
+            (late, 0, {"ty": ty_prev}, send_c.at[n, 0:5], recv_c.at[n, 0:5]),
+            (early, 1, {"ty": ty_next}, send_d.at[n, 0:6], recv_d.at[n, 0:6]),
+            (late, 1, {"ty": ty_next}, send_d.at[n, 0:5], recv_d.at[n, 0:5]),
+            (first, 2, low_high, send_a.at[n], recv_back_up.at[n]),
+            (later, 2, low_high, send_a.at[n, 2:4], recv_back_up.at[n, 2:4]),
+            (first, 3, high_low, send_b.at[n, 0:3], recv_ahead_down.at[n]),
+            (later, 3, high_low, send_b.at[n, 1:3], recv_ahead_down.at[n, 1:3]),
+            (before_last, 4, low_low, send_a.at[n, 0:2], recv_ahead_up.at[n]),
+            (before_last, 5, high_high, send_b.at[n, 3:5], recv_back_down.at[n]),
+            (always, 6, {"tx": tx_prev}, send_a.at[n], recv_a.at[n]),
+            (always, 7, {"tx": tx_next}, send_b.at[n, 1:5], recv_b.at[n]),
         )
         return [
-            remote(src, dst, (send_sem.at[n, i], recv_sem.at[n, i]), target)
-            for i, (target, src, dst) in enumerate(ways)
+            (when, remote(src, dst, (send_sem.at[n, i], recv_sem.at[n, i]), target))
+            for when, i, target, src, dst in ways
         ]
+
+    def each_trace(n, act):
+        for when, copy in trace_copies(n):
+            if when is None:
+                act(copy)
+            else:
+
+                @pl.when(when)
+                def _(copy=copy):
+                    act(copy)
+
+    def clear(ref):
+        ref[...] = jnp.zeros(ref.shape, jnp.float32)
+
+    clear(recv_c.at[2:STEPS, 5])
+    clear(recv_d.at[2:STEPS, 5])
+    clear(recv_ahead_up.at[STEPS - 1])
+    clear(recv_back_down.at[STEPS - 1])
 
     load.wait()
     pl.semaphore_wait(barrier, len(partners))
-    for copy in medium_copies():
-        copy.start()
 
     def alone_step(n, carry):
         depth_first, depth_last = depth == 0, depth == NZ - 1
@@ -286,21 +323,38 @@
                 alone[r, 3, :, part(k)] = hx
                 alone[r, 4, :, part(k)] = hy
                 alone[r, 5, :, part(k)] = hz
-                send_x[n, 2 * r : 2 * r + 1, part(k)] = ey[k][0:1]
-                send_x[n, 2 * r + 1 : 2 * r + 2, part(k)] = ez[k][0:1]
-                send_x[n, 4 + 2 * r : 5 + 2 * r, part(k)] = hy[rows - 1 : rows]
-                send_x[n, 5 + 2 * r : 6 + 2 * r, part(k)] = hz[rows - 1 : rows]
+                e_edge = (ey[k][0:1], ez[k][0:1])
+                h_edge = (hy[rows - 1 : rows], hz[rows - 1 : rows])
+                side, tile, beside = (
+                    (send_c, 4 + k, 0) if k < chunks // 2 else (send_d, 3 + chunks - k, 3)
+                )
+                for c in range(2):
+                    i, j = 4 * (k % 2) + 2 * r + c, 2 * r + c
+                    send_a[n, beside, i : i + 1] = e_edge[c]
+                    send_b[n, beside + 1, i : i + 1] = h_edge[c]
+                    side[n, tile, j : j + 1] = e_edge[c]
+                    side[n, tile, 4 + j : 5 + j] = h_edge[c]
+                spot = slice(4 * r, 4 * r + 4)
                 if k == 0:
-                    send_y[n, r, :, 0:LANES] = jnp.where(low, ex[k], roll(ez[k], NZ, 1))
+                    line = jnp.where(low, ex[k], roll(ez[k], NZ, 1))
+                    upper, lower = line[0:8], line[8:16]
+                    send_c[n, 2 * r], send_c[n, 2 * r + 1] = upper, lower
+                    send_a[n, 1, spot] = (upper if r == 0 else roll(upper, 4, 0))[spot]
+                    send_b[n, 2, spot] = (roll(lower, 4, 0) if r == 0 else lower)[spot]
+                    send_b[n, 0, spot] = (lower if r == 0 else roll(lower, 4, 0))[spot]
                 if k == chunks - 1:
-                    send_y[n, r, :, LANES : 2 * LANES] = jnp.where(low, roll(hx, NZ, 1), hz)
-
-        for copy in trace_copies(n):
-            copy.start()
+                    line = jnp.where(low, roll(hx, NZ, 1), hz)
+                    upper, lower = line[0:8], line[8:16]
+                    send_d[n, 2 * r], send_d[n, 2 * r + 1] = upper, lower
+                    send_a[n, 2, spot] = (upper if r == 0 else roll(upper, 4, 0))[spot]
+                    send_b[n, 3, spot] = (roll(lower, 4, 0) if r == 0 else lower)[spot]
+
+        each_trace(n, lambda copy: copy.start())
 
         @pl.when(n == 0)
         def _():
-            for copy in far_copies():
+            prepare()
+            for copy in medium_copies():
                 copy.start()
 
         @pl.when(n < STEPS - 1)
@@ -340,6 +394,11 @@
 
     lax.fori_loop(0, STEPS, alone_step, 0)
 
+    for copy in medium_copies():
+        copy.wait_recv()
+    for copy in shared_copies(core):
+        copy.start()
+
     load_wide.wait()
     for r in range(2):
         for c in range(12):
@@ -349,7 +408,7 @@
                 else:
                     wide[r, c, :, part(k)] = jnp.zeros((wide_rows, LANES), jnp.float32)
 
-    for copy in medium_copies():
+    for copy in shared_copies(1 - core):
         copy.wait_recv()
     row_id, lane_id, low, depth = ids(wide_rows)
     near_row = jnp.where(row_id < rows + REACH, row_id, row_id - wide_rows)
@@ -364,20 +423,53 @@
             coefs[i, :, part(k)] = made[i]
         coefs[4, :, part(k)] = jnp.where(present, time_step, 0.0)
 
-    for copy in far_copies():
-        copy.wait_recv()
-
     def wide_step(n, carry):
         depth_first, depth_last = depth == 0, depth == NZ - 1
         start = jnp.where(n == 0, 1.0, 0.0)
-        for copy in trace_copies(n):
-            copy.wait_recv()
+
+        @pl.when(n == STEPS - 1)
+        def _():
+            for k in range(chunks):
+                value = jnp.zeros((rows, LANES), jnp.float32)
+                for i in range(1, STEPS - 1):
+                    for c in range(3):
+                        value = value + duals[STEPS - 1 - i, c, :, part(k)] * moves[i, c, :, part(k)]
+                partial[:, part(k)] = value
+
+        each_trace(n, lambda copy: copy.wait_recv())
 
         def get(r, c):
             return [wide[r, c, :, part(k)] for k in range(wide_chunks)]
 
+        def pair(up, down, r):
+            up = up if r == 0 else roll(up, 4, 0)
+            down = roll(down, 4, 0) if r == 0 else down
+            return jnp.where(row_id[0:8] < 4, up, down)
+
         def tall(v):
             return jnp.concatenate([jnp.zeros((rows, LANES), jnp.float32), v], axis=0)
+
+        def x_ahead(k, i):
+            tile = (
+                recv_a.at[n, 3 * (k // 2)]
+                if k < chunks
+                else (recv_ahead_up.at[n, 0] if k < chunks + 2 else recv_back_up.at[n, 3])
+            )
+            i = i + 4 * (k % 2)
+            return keep_x_next * tile[i : i + 1]
+
+        def x_back(k, i):
+            tile = (
+                recv_b.at[n, 3 * (k // 2)]
+                if k < chunks
+                else (recv_ahead_down.at[n, 1] if k < chunks + 2 else recv_back_down.at[n, 1])
+            )
+            i = i + 4 * (k % 2)
+            return keep_x_prev * tile[i : i + 1]
+
+        def x_corner(k, i):
+            tile = recv_c.at[n, k] if k < chunks + 2 else recv_d.at[n, 3 + wide_chunks - k]
+            return tile[i : i + 1]
 
         def at_row(i, v):
             return jnp.where(row_id == i, v, 0.0)
@@ -413,22 +505,28 @@
         zero = jnp.zeros((wide_rows, LANES), jnp.float32)
         for r in range(2):
             def x_up(v, k, c):
-                out = roll(v, -1, 0) + at_row(rows - 1, keep_x_next * recv_x[n, 2 * r + c : 2 * r + c + 1, part(k)])
+                out = roll(v, -1, 0) + at_row(rows - 1, x_ahead(k, 2 * r + c))
                 if k >= chunks:
-                    out = out + at_row(wide_rows - 1, recv_xc[n, 2 * r + c : 2 * r + c + 1, part(k - chunks)])
+                    out = out + at_row(wide_rows - 1, x_corner(k, 2 * r + c))
                 return out
 
             def x_down(v, k, c, far):
-                i = 4 + 2 * r + c
                 out = jnp.where(row_id == rows + REACH, far, roll(v, 1, 0))
-                out = out + at_row(0, keep_x_prev * recv_x[n, i : i + 1, part(k)])
+                out = out + at_row(0, x_back(k, 2 * r + c))
                 if k >= chunks:
-                    out = out + at_row(rows, recv_xc[n, i : i + 1, part(k - chunks)])
+                    out = out + at_row(rows, x_corner(k, 4 + 2 * r + c))
                 return out
 
             ex, ey, ez = get(r, 0), get(r, 1), get(r, 2)
-            got = recv_ye[n, r] * keep_y_next
-            corner = tall(recv_yc[n, r, :, 0:LANES])
+            got = keep_y_next * jnp.concatenate(
+                [
+                    recv_c[n, 2 * r],
+                    recv_c[n, 2 * r + 1],
+                    pair(recv_ahead_up[n, 1], recv_ahead_down[n, 2], r),
+                ],
+                axis=0,
+            )
+            corner = tall(pair(recv_a[n, 1], recv_b[n, 1], r))
             y_ez = y_up(ez, got, corner)
             y_ex = y_up(ex, roll(got, NZ, 1), roll(corner, NZ, 1))
             for k in range(wide_chunks):
@@ -444,18 +542,25 @@
                     wide[r, 3 + c, :, part(k)] = wide[r, 3 + c, :, part(k)] - coefs[4, :, part(k)] * curls[c]
 
             hx, hy, hz = get(r, 3), get(r, 4), get(r, 5)
-            got = recv_yh[n, r] * keep_y_prev
-            corner = tall(recv_yc[n, r, :, LANES : 2 * LANES])
+            got = keep_y_prev * jnp.concatenate(
+                [
+                    recv_d[n, 2 * r],
+                    recv_d[n, 2 * r + 1],
+                    pair(recv_back_up[n, 2], recv_back_down[n, 0], r),
+                ],
+                axis=0,
+            )
+            corner = tall(pair(recv_a[n, 2], recv_b[n, 2], r))
             far_line = at_row(
-                rows - 1, (-time_step * start * keep_x_next) * roll(far_x[2 * r : 2 * r + 1], NZ, 1)
+                rows - 1, (-time_step * start * keep_x_next) * roll(recv_back_up[0, 0, 4 + 2 * r : 5 + 2 * r], NZ, 1)
             )
             far_row = jnp.where(
-                low[0:1], 0.0, (time_step * start * keep_y_next) * roll(far_y[r, REACH - 1 : REACH], NZ, 1)
+                low[0:1], 0.0, (time_step * start * keep_y_next) * roll(recv_ahead_down[0, 0, 4 * r + 3 : 4 * r + 4], NZ, 1)
             )
             y_hx = y_down(hx, got, corner, zero)
             y_hz = y_down(hz, roll(got, NZ, 1), roll(corner, NZ, 1), far_line)
             amount = waveforms[0, r, n]
-            for k in range(wide_chunks):
+            def electric(k):
                 x_hz = x_down(hz[k], k, 1, far_row if k == chunks - 1 else 0.0)
                 x_hy = x_down(hy[k], k, 0, 0.0)
                 z_hy = jnp.where(depth_first, 0.0, roll(hy[k], 1, 1))
@@ -480,63 +585,76 @@
                         else:
                             duals[n, c, :, part(k)] = new[0:rows]
                     wide[r, c, :, part(k)] = new
+            for k in range(chunks):
+                electric(k)
+
+            @pl.when(n < STEPS - 1)
+            def _():
+                for k in range(chunks, wide_chunks):
+                    electric(k)
+
         return carry
 
     lax.fori_loop(0, STEPS, wide_step, 0)
 
     store = pltpu.make_async_copy(wide.at[:, 0:3, 0:rows, 0:flat], final_out.at[0], store_sem.at[0])
     store.start()
-
-    for k in range(chunks):
-        value = jnp.zeros((rows, LANES), jnp.float32)
-        for n in range(STEPS):
-            for c in range(3):
-                value = value + duals[STEPS - 1 - n, c, :, part(k)] * moves[n, c, :, part(k)]
-        partial[:, part(k)] = value
 
     half = rows // 2
     mine = pl.ds(pl.multiple_of(core * half, half), half)
     other = pl.ds(pl.multiple_of((1 - core) * half, half), half)
-
-    def wave_copy(i, src, dst, target):
-        return pltpu.make_async_remote_copy(
-            src_ref=src,
-            dst_ref=dst,
-            send_sem=wave_send_sem.at[i],
-            recv_sem=wave_recv_sem.at[i],
-            device_id={"wave": target},
-            device_id_type=MESH,
-        )
-
-    swap = wave_copy(0, partial.at[other], core_in, wave_core)
-    swap.start()
-    swap.wait_recv()
-    half_sum[...] = partial[mine, :] + core_in[...]
-    cross = wave_copy(1, half_sum, chip_in, wave_chip)
-    cross.start()
-    cross.wait_recv()
-    total[mine, :] = (contrast * inside[mine, :]) * (half_sum[...] + chip_in[...])
-    back = wave_copy(2, total.at[mine], total.at[mine], wave_core)
-    back.start()
-    back.wait_recv()
-    grad = pltpu.make_async_copy(total, grad_out, store_sem.at[1])
-    grad.start()
-
-    swap.wait_send()
-    cross.wait_send()
-    back.wait_send()
-
-    for copy in medium_copies() + far_copies():
+    pieces = [slice(0, flat // 2), slice(flat // 2, flat)]
+
+    def wave_copies(i, src, dst, target):
+        return [
+            remote(src(piece), dst(piece), (wave_send_sem.at[i, j], wave_recv_sem.at[i, j]), {"wave": target})
+            for j, piece in enumerate(pieces)
+        ]
+
+    swap = wave_copies(0, lambda p: partial.at[other, p], lambda p: core_in.at[:, p], wave_core)
+    cross = wave_copies(1, lambda p: half_sum.at[:, p], lambda p: chip_in.at[:, p], wave_chip)
+    back = wave_copies(2, lambda p: grad_out.at[mine, p], lambda p: grad_out.at[mine, p], wave_core)
+    for j in range(2):
+        for k in range(j * chunks // 2, (j + 1) * chunks // 2):
+            value = partial[:, part(k)]
+            for i in (0, STEPS - 1):
+                for c in range(3):
+                    value = value + duals[STEPS - 1 - i, c, :, part(k)] * moves[i, c, :, part(k)]
+            partial[:, part(k)] = value
+        swap[j].start()
+    for j, p in enumerate(pieces):
+        swap[j].wait_recv()
+        half_sum[:, p] = partial[mine, p] + core_in[:, p]
+        cross[j].start()
+    for j, p in enumerate(pieces):
+        cross[j].wait_recv()
+        grad_out[mine, p] = (contrast * inside[mine, p]) * (half_sum[:, p] + chip_in[:, p])
+        back[j].start()
+    for j in range(2):
+        back[j].wait_recv()
+    for copy in swap + cross + back:
         copy.wait_send()
 
+    for copy in medium_copies() + shared_copies(core):
+        copy.wait_send()
+
     def drain(n, carry):
-        for copy in trace_copies(n):
-            copy.wait_send()
+        each_trace(n, lambda copy: copy.wait_send())
         return carry
 
     lax.fori_loop(0, STEPS, drain, 0)
     store.wait()
-    grad.wait()
+
+
+def put_out(grad, final, grad_out, final_out, sem):
+    copies = (
+        pltpu.make_async_copy(final, final_out, sem.at[0]),
+        pltpu.make_async_copy(grad, grad_out, sem.at[1]),
+    )
+    for copy in copies:
+        copy.start()
+    for copy in copies:
+        copy.wait()
 
 
 def solution(mesh):
@@ -546,16 +664,13 @@
         rows, flat = material_map.shape
         f32 = jnp.float32
         vmem, smem, anywhere = pltpu.VMEM, pltpu.SMEM, pl.ANY
-        spaces = (anywhere, anywhere, smem, vmem, vmem, smem, smem, smem)
+        spaces = (anywhere,) * 8
         wide_rows, wide_flat = rows + 2 * REACH, flat + 2 * REACH * NZ
-        return pl.pallas_call(
+        grad, final = pl.pallas_call(
             functools.partial(kernel, (n_wave, n_tx, n_ty, rows, flat)),
-            out_shape=(
-                jax.ShapeDtypeStruct((rows, flat), f32),
-                jax.ShapeDtypeStruct((1, 2, 3, rows, flat), f32),
-            ),
+            out_shape=(vmem((rows, flat), f32), vmem((1, 2, 3, rows, flat), f32)),
             in_specs=[pl.BlockSpec(memory_space=space) for space in spaces],
-            out_specs=(pl.BlockSpec(memory_space=anywhere),) * 2,
+            out_specs=(pl.BlockSpec(memory_space=vmem),) * 2,
             scratch_shapes=[
                 vmem((2, 12, rows, flat), f32),
                 vmem((2, 12, wide_rows, wide_flat), f32),
@@ -566,31 +681,40 @@
                 vmem((rows, flat), f32),
                 vmem((STEPS, 3, rows, flat), f32),
                 vmem((STEPS, 3, rows, flat), f32),
-                vmem((STEPS, 2, rows, 2 * LANES), f32),
-                vmem((STEPS, 8, flat), f32),
-                vmem((STEPS, 2, wide_rows, LANES), f32),
-                vmem((STEPS, 2, wide_rows, LANES), f32),
-                vmem((STEPS, 2, 2 * REACH, 2 * LANES), f32),
-                vmem((STEPS, 8, wide_flat), f32),
-                vmem((STEPS, 8, 2 * REACH * NZ), f32),
-                vmem((8, LANES), f32),
-                vmem((2, 8, LANES), f32),
+                *(vmem((STEPS, tiles, 8, LANES), f32) for tiles in (4, 5, 6, 6)),
+                *(vmem((STEPS, tiles, 8, LANES), f32) for tiles in (4, 4, 6, 6, 2, 3, 4, 2)),
+                smem(waveforms.shape, f32),
+                vmem((rows, flat), jnp.int32),
+                vmem((rows, flat), f32),
+                smem(table.shape, f32),
+                smem(planes.shape, jnp.int32),
+                smem(box.shape, jnp.int32),
                 vmem((rows, flat), f32),
                 vmem((rows // 2, flat), f32),
                 vmem((rows // 2, flat), f32),
                 vmem((rows // 2, flat), f32),
-                vmem((rows, flat), f32),
                 pltpu.SemaphoreType.DMA((STEPS, FLOWS)),
                 pltpu.SemaphoreType.DMA((STEPS, FLOWS)),
                 pltpu.SemaphoreType.DMA((10,)),
                 pltpu.SemaphoreType.DMA((10,)),
-                pltpu.SemaphoreType.DMA((3,)),
-                pltpu.SemaphoreType.DMA((3,)),
-                pltpu.SemaphoreType.DMA((3,)),
+                pltpu.SemaphoreType.DMA((3, 2)),
+                pltpu.SemaphoreType.DMA((3, 2)),
+                pltpu.SemaphoreType.DMA((10,)),
                 pltpu.SemaphoreType.DMA((2,)),
             ],
             compiler_params=pltpu.CompilerParams(collective_id=0, has_side_effects=True),
         )(fields, jnp.transpose(profiles, (0, 2, 1, 3)), waveforms, material_map, density, table, planes, box)
+        return pl.pallas_call(
+            put_out,
+            out_shape=(
+                jax.ShapeDtypeStruct((rows, flat), f32),
+                jax.ShapeDtypeStruct((1, 2, 3, rows, flat), f32),
+            ),
+            in_specs=[pl.BlockSpec(memory_space=vmem)] * 2,
+            out_specs=(pl.BlockSpec(memory_space=anywhere),) * 2,
+            scratch_shapes=[pltpu.SemaphoreType.DMA((2,))],
+            compiler_params=pltpu.CompilerParams(vmem_limit_bytes=1 << 20),
+        )(grad, final)
 
     placed = (
         P("wave", None, None, "tx", "ty"),

time: 44.2 us -> 38.7 us (0.88)
  local copies, waits for them, and re-layouts: 2.99 us -> 0 us
  Pallas kernels: 40.3 us -> 37.9 us
    pallas_call x1, Pallas kernels: 40.3 us -> 37.2 us  [on_device(): pl.pallas_call(functools.partial(kernel, (n_wave, n_tx, n_ty, rows, flat)...]
    unnamed x2 -> x0, local copies, waits for them, and re-layouts: 2.99 us -> none
    pallas_call x0 -> x1, Pallas kernels: none -> 0.7 us  [on_device(): pl.pallas_call(put_out, out_shape=(jax.ShapeDtypeStruct((rows, flat), f32...]
where the time goes in v3:
time: 38.7 us; the launch traced here: 38.5 us
  Pallas kernels  37.9 us (98%)
  between operations  0.64 us (2%)
    pallas_call x1, Pallas kernels, on_device(): pl.pallas_call(functools.partial(kernel, (n_wave, n_tx, n_ty, rows, flat)...  37.2 us

profile of v3, /device:TPU:1, one launch (start us, length us, event | category | flops | bytes accessed | tf_op | source)
XLA Modules:
  0.0 38.5 jit_solution(18117817922904705240)
XLA Ops:
  0.6 37.2 %shard_map.95 = (f32[16,512]{1,0:T(8,128)S(1)}, f32[1,2,3,16,512]{4,3,2,1,0:T(8,128)S(1)}) custom-call(f32[1,2,12,16,512]{4,3,2,1,0:T(8,128)} %fields.1, f32[1,3,2,8192]{3,2,1,0:T(2,128)} %bitcast.1, f32[1,2,5]{2,1,0:T(2,128)} %waveforms_in.1, s32[16,512]{1,0:T(8,128)} %material_in.1, f32[16,512]{1,0:T(8,128)} %density_in.1, f32[3,4]{1,0:T(4,128)} %table_in.1, ...), custom_call_target="tpu_custom_call" | custom-call | tf_op jit(solution)/shard_map/pallas_call | solution.py:669
  37.9 0.7 %shard_map.96 = (f32[16,512]{1,0:T(8,128)}, f32[1,2,3,16,512]{4,3,2,1,0:T(8,128)}) custom-call(f32[16,512]{1,0:T(8,128)S(1)} %get-tuple-element.4.grad, f32[1,2,3,16,512]{4,3,2,1,0:T(8,128)S(1)} %get-tuple-element.5.final), custom_call_target="tpu_custom_call" | custom-call | tf_op jit(solution)/shard_map/pallas_call | solution.py:707

commit v4 on v3

--- a/solution.py
+++ b/solution.py
@@ -70,6 +70,7 @@
     wave_recv_sem,
     load_sem,
     store_sem,
+    answer,
 ):
     n_wave, n_tx, n_ty, rows, flat = sizes
     chunks = flat // LANES
@@ -109,27 +110,65 @@
     for copy in small:
         copy.start()
     load_wide = pltpu.make_async_copy(fields.at[0], wide.at[:, :, 0:rows, 0:flat], load_sem.at[2])
-    load_wide.start()
 
     barrier = pltpu.get_barrier_semaphore()
     low_low = {"tx": tx_prev, "ty": ty_prev}
     low_high = {"tx": tx_prev, "ty": ty_next}
     high_low = {"tx": tx_next, "ty": ty_prev}
     high_high = {"tx": tx_next, "ty": ty_next}
-    partners = (
-        {"ty": ty_prev},
-        {"ty": ty_next},
-        low_low,
-        low_high,
-        high_low,
-        high_high,
-        {"tx": tx_prev},
-        {"tx": tx_next},
-        {"wave": wave_chip},
-        {"wave": wave_core},
-    )
-    for partner in partners:
-        pl.semaphore_signal(barrier, inc=1, device_id=partner, device_id_type=MESH)
+    far_half = wave // 2
+    more_x, less_x = tx < n_tx - 1, tx > 0
+    more_y, less_y = ty < n_ty - 1, ty > 0
+    around = {
+        "y_prev": ({"ty": ty_prev}, less_y, more_y),
+        "y_next": ({"ty": ty_next}, more_y, less_y),
+        "x_prev": ({"tx": tx_prev}, less_x, more_x),
+        "x_next": ({"tx": tx_next}, more_x, less_x),
+        "low_low": (low_low, less_x & less_y, more_x & more_y),
+        "low_high": (low_high, less_x & more_y, more_x & less_y),
+        "high_low": (high_low, more_x & less_y, less_x & more_y),
+        "high_high": (high_high, more_x & more_y, less_x & less_y),
+    }
+
+    def clear(ref):
+        ref[...] = jnp.zeros(ref.shape, jnp.float32)
+
+    clear(recv_c.at[2:STEPS, 5])
+    clear(recv_d.at[2:STEPS, 5])
+    clear(recv_ahead_up.at[STEPS - 1])
+    clear(recv_back_down.at[STEPS - 1])
+    for name, ref in (
+        ("y_prev", recv_c),
+        ("y_next", recv_d),
+        ("x_prev", recv_a),
+        ("x_next", recv_b),
+        ("low_low", recv_ahead_up),
+        ("low_high", recv_back_up),
+        ("high_low", recv_ahead_down),
+        ("high_high", recv_back_down),
+    ):
+
+        @pl.when(jnp.logical_not(around[name][2]))
+        def _(ref=ref):
+            clear(ref)
+
+    @pl.when(jnp.logical_not(more_x & less_x & more_y & less_y))
+    def _():
+        clear(medium.at[:, rows:wide_rows])
+        clear(medium.at[:, 0:rows, flat : 2 * flat])
+
+    @pl.when(far_half == 0)
+    def _():
+        pl.semaphore_signal(barrier, inc=1, device_id={"wave": wave_chip}, device_id_type=MESH)
+
+    pl.semaphore_signal(barrier, inc=1, device_id={"wave": wave_core}, device_id_type=MESH)
+    greetings = far_half + 1
+    for target, there, _ in around.values():
+        greetings = greetings + jnp.where(there, 1, 0)
+
+        @pl.when(there)
+        def _(target=target):
+            pl.semaphore_signal(barrier, inc=1, device_id=target, device_id_type=MESH)
 
     def ids(count):
         row = lax.broadcasted_iota(jnp.int32, (count, LANES), 0)
@@ -155,11 +194,9 @@
         drive = omega * omega * time_step / denom
         return reach, (1.0 - 0.25 * damping) / denom, drive, drive * spread
 
-    def prepare():
-        for copy in small:
+    def make_medium():
+        for copy in small[:4]:
             copy.wait()
-        load_rest.wait()
-        load_profile.wait()
         for k in range(chunks):
             material = material_map[:, part(k)]
             eps = per_material(material, [table[m, 0] for m in range(NMAT)])
@@ -177,6 +214,13 @@
             inside[:, part(k)] = within
             medium[0, 0:rows, part(k)] = time_step / (eps + (within * density[:, part(k)]) * contrast)
             medium[1, 0:rows, part(k)] = material.astype(jnp.float32)
+
+    def prepare():
+        for copy in small[4:]:
+            copy.wait()
+        load_wide.start()
+        load_rest.wait()
+        load_profile.wait()
         for k in range(chunks):
             made = coefficients(medium[0, 0:rows, part(k)], material_map[:, part(k)])
             for i in range(4):
@@ -190,11 +234,6 @@
                         coefs[0, 0:rows, part(k)] * on_plane * profile[c, r : r + 1, part(k)]
                     )
                     source[r, c, rows:wide_rows, part(k)] = jnp.zeros((2 * REACH, LANES), jnp.float32)
-
-    keep_x_next = jnp.where(tx == n_tx - 1, 0.0, 1.0)
-    keep_x_prev = jnp.where(tx == 0, 0.0, 1.0)
-    keep_y_next = jnp.where(ty == n_ty - 1, 0.0, 1.0)
-    keep_y_prev = jnp.where(ty == 0, 0.0, 1.0)
 
     def roll(v, shift, axis):
         return pltpu.roll(v, shift % v.shape[axis], axis)
@@ -215,25 +254,39 @@
     beyond, ahead_of = slice(flat, flat + edge), slice(flat + edge, flat + 2 * edge)
     whole, inner = slice(0, rows), slice(0, flat)
 
+    def guarded(act, ways, sending):
+        for name, active, copy in ways:
+            when = around[name][1 if sending else 2]
+            if active is not None:
+                when = when & active
+
+            @pl.when(when)
+            def _(copy=copy):
+                act(copy)
+
     def medium_copies():
         ways = (
-            ({"ty": ty_prev}, whole, left, whole, beyond),
-            ({"ty": ty_next}, whole, right, whole, ahead_of),
-            (low_low, top, left, after, beyond),
-            (low_high, top, right, after, ahead_of),
-            (high_low, bottom, left, before, beyond),
-            (high_high, bottom, right, before, ahead_of),
-            ({"tx": tx_prev}, top, inner, after, inner),
-            ({"tx": tx_next}, bottom, inner, before, inner),
+            ("y_prev", whole, left, whole, beyond),
+            ("y_next", whole, right, whole, ahead_of),
+            ("low_low", top, left, after, beyond),
+            ("low_high", top, right, after, ahead_of),
+            ("high_low", bottom, left, before, beyond),
+            ("high_high", bottom, right, before, ahead_of),
+            ("x_prev", top, inner, after, inner),
+            ("x_next", bottom, inner, before, inner),
         )
         return [
-            remote(
-                medium.at[core, a, b],
-                medium.at[core, c, d],
-                (once_send_sem.at[i], once_recv_sem.at[i]),
-                target,
+            (
+                name,
+                None,
+                remote(
+                    medium.at[core, a, b],
+                    medium.at[core, c, d],
+                    (once_send_sem.at[i], once_recv_sem.at[i]),
+                    around[name][0],
+                ),
             )
-            for i, (target, a, b, c, d) in enumerate(ways)
+            for i, (name, a, b, c, d) in enumerate(ways)
         ]
 
     def shared_copies(plane):
@@ -249,47 +302,35 @@
         ]
 
     def trace_copies(n):
-        always, first, later = None, n == 0, n > 0
-        early, late, before_last = n < 2, n >= 2, n < STEPS - 1
+        first, later, early, late, before_last = n == 0, n > 0, n < 2, n >= 2, n < STEPS - 1
         ways = (
-            (early, 0, {"ty": ty_prev}, send_c.at[n, 0:6], recv_c.at[n, 0:6]),
-            (late, 0, {"ty": ty_prev}, send_c.at[n, 0:5], recv_c.at[n, 0:5]),
-            (early, 1, {"ty": ty_next}, send_d.at[n, 0:6], recv_d.at[n, 0:6]),
-            (late, 1, {"ty": ty_next}, send_d.at[n, 0:5], recv_d.at[n, 0:5]),
-            (first, 2, low_high, send_a.at[n], recv_back_up.at[n]),
-            (later, 2, low_high, send_a.at[n, 2:4], recv_back_up.at[n, 2:4]),
-            (first, 3, high_low, send_b.at[n, 0:3], recv_ahead_down.at[n]),
-            (later, 3, high_low, send_b.at[n, 1:3], recv_ahead_down.at[n, 1:3]),
-            (before_last, 4, low_low, send_a.at[n, 0:2], recv_ahead_up.at[n]),
-            (before_last, 5, high_high, send_b.at[n, 3:5], recv_back_down.at[n]),
-            (always, 6, {"tx": tx_prev}, send_a.at[n], recv_a.at[n]),
-            (always, 7, {"tx": tx_next}, send_b.at[n, 1:5], recv_b.at[n]),
+            ("y_prev", early, 0, send_c.at[n, 0:6], recv_c.at[n, 0:6]),
+            ("y_prev", late, 0, send_c.at[n, 0:5], recv_c.at[n, 0:5]),
+            ("y_next", early, 1, send_d.at[n, 0:6], recv_d.at[n, 0:6]),
+            ("y_next", late, 1, send_d.at[n, 0:5], recv_d.at[n, 0:5]),
+            ("low_high", first, 2, send_a.at[n], recv_back_up.at[n]),
+            ("low_high", later, 2, send_a.at[n, 2:4], recv_back_up.at[n, 2:4]),
+            ("high_low", first, 3, send_b.at[n, 0:3], recv_ahead_down.at[n]),
+            ("high_low", later, 3, send_b.at[n, 1:3], recv_ahead_down.at[n, 1:3]),
+            ("low_low", before_last, 4, send_a.at[n, 0:2], recv_ahead_up.at[n]),
+            ("high_high", before_last, 5, send_b.at[n, 3:5], recv_back_down.at[n]),
+            ("x_prev", None, 6, send_a.at[n], recv_a.at[n]),
+            ("x_next", None, 7, send_b.at[n, 1:5], recv_b.at[n]),
         )
         return [
-            (when, remote(src, dst, (send_sem.at[n, i], recv_sem.at[n, i]), target))
-            for when, i, target, src, dst in ways
+            (name, active, remote(src, dst, (send_sem.at[n, i], recv_sem.at[n, i]), around[name][0]))
+            for name, active, i, src, dst in ways
         ]
 
-    def each_trace(n, act):
-        for when, copy in trace_copies(n):
-            if when is None:
-                act(copy)
-            else:
-
-                @pl.when(when)
-                def _(copy=copy):
-                    act(copy)
-
-    def clear(ref):
-        ref[...] = jnp.zeros(ref.shape, jnp.float32)
-
-    clear(recv_c.at[2:STEPS, 5])
-    clear(recv_d.at[2:STEPS, 5])
-    clear(recv_ahead_up.at[STEPS - 1])
-    clear(recv_back_down.at[STEPS - 1])
-
+    make_medium()
+    pl.semaphore_wait(barrier, greetings)
+
+    @pl.when(far_half == 1)
+    def _():
+        pl.semaphore_signal(answer, inc=1, device_id={"wave": wave_chip}, device_id_type=MESH)
+
+    guarded(lambda copy: copy.start(), medium_copies(), True)
     load.wait()
-    pl.semaphore_wait(barrier, len(partners))
 
     def alone_step(n, carry):
         depth_first, depth_last = depth == 0, depth == NZ - 1
@@ -349,13 +390,11 @@
                     send_a[n, 2, spot] = (upper if r == 0 else roll(upper, 4, 0))[spot]
                     send_b[n, 3, spot] = (roll(lower, 4, 0) if r == 0 else lower)[spot]
 
-        each_trace(n, lambda copy: copy.start())
+        guarded(lambda copy: copy.start(), trace_copies(n), True)
 
         @pl.when(n == 0)
         def _():
             prepare()
-            for copy in medium_copies():
-                copy.start()
 
         @pl.when(n < STEPS - 1)
         def _():
@@ -394,8 +433,7 @@
 
     lax.fori_loop(0, STEPS, alone_step, 0)
 
-    for copy in medium_copies():
-        copy.wait_recv()
+    guarded(lambda copy: copy.wait_recv(), medium_copies(), False)
     for copy in shared_copies(core):
         copy.start()
 
@@ -436,10 +474,7 @@
                         value = value + duals[STEPS - 1 - i, c, :, part(k)] * moves[i, c, :, part(k)]
                 partial[:, part(k)] = value
 
-        each_trace(n, lambda copy: copy.wait_recv())
-
-        def get(r, c):
-            return [wide[r, c, :, part(k)] for k in range(wide_chunks)]
+        guarded(lambda copy: copy.wait_recv(), trace_copies(n), False)
 
         def pair(up, down, r):
             up = up if r == 0 else roll(up, 4, 0)
@@ -456,7 +491,7 @@
                 else (recv_ahead_up.at[n, 0] if k < chunks + 2 else recv_back_up.at[n, 3])
             )
             i = i + 4 * (k % 2)
-            return keep_x_next * tile[i : i + 1]
+            return tile[i : i + 1]
 
         def x_back(k, i):
             tile = (
@@ -465,60 +500,63 @@
                 else (recv_ahead_down.at[n, 1] if k < chunks + 2 else recv_back_down.at[n, 1])
             )
             i = i + 4 * (k % 2)
-            return keep_x_prev * tile[i : i + 1]
+            return tile[i : i + 1]
 
         def x_corner(k, i):
             tile = recv_c.at[n, k] if k < chunks + 2 else recv_d.at[n, 3 + wide_chunks - k]
             return tile[i : i + 1]
 
-        def at_row(i, v):
-            return jnp.where(row_id == i, v, 0.0)
-
-        def y_up(vs, inner_edge, outer_edge):
-            turned = [roll(v, NZ, 1) for v in vs]
-            out = []
-            for k in range(wide_chunks):
-                other = turned[(k + 1) % wide_chunks]
-                if k == chunks - 1:
-                    other = other + inner_edge
-                if k == chunks + chunks // 2 - 1:
-                    other = jnp.zeros_like(other)
-                if k == wide_chunks - 1:
-                    other = other + outer_edge
-                out.append(jnp.where(low, turned[k], other))
+        def edit(v, i, change):
+            groups = [v[8 * g : 8 * g + 8] for g in range(wide_rows // 8)]
+            g = i // 8
+            groups[g] = jnp.where(row_id[0:8] == i % 8, change(groups[g]), groups[g])
+            return jnp.concatenate(groups, axis=0)
+
+        class Turned:
+            def __init__(self, r, c):
+                self.r, self.c, self.held = r, c, {}
+
+            def __getitem__(self, k):
+                k = k % wide_chunks
+                if k not in self.held:
+                    self.held[k] = roll(wide[self.r, self.c, :, part(k)], NZ, 1)
+                return self.held[k]
+
+        def y_up(turned, k, inner_edge, outer_edge):
+            if k == chunks + chunks // 2 - 1:
+                return jnp.where(low, turned[k], 0.0)
+            other = turned[k + 1]
+            if k == chunks - 1:
+                other = other + inner_edge
+            if k == wide_chunks - 1:
+                other = other + outer_edge
+            return jnp.where(low, turned[k], other)
+
+        def y_down(turned, k, inner_edge, outer_edge, far):
+            if k == chunks + chunks // 2:
+                return jnp.where(low, far, turned[k])
+            other = turned[k - 1]
+            if k == 0:
+                other = other + inner_edge
+            if k == chunks:
+                other = other + outer_edge
+            return jnp.where(low, other, turned[k])
+
+        def x_up(v, k, i):
+            out = edit(roll(v, -1, 0), rows - 1, lambda g: g + x_ahead(k, i))
+            if k >= chunks:
+                out = edit(out, wide_rows - 1, lambda g: g + x_corner(k, i))
             return out
 
-        def y_down(vs, inner_edge, outer_edge, far):
-            turned = [roll(v, NZ, 1) for v in vs]
-            out = []
-            for k in range(wide_chunks):
-                other = turned[(k - 1) % wide_chunks]
-                if k == 0:
-                    other = other + inner_edge
-                if k == chunks:
-                    other = other + outer_edge
-                if k == chunks + chunks // 2:
-                    other = far
-                out.append(jnp.where(low, other, turned[k]))
+        def x_down(v, k, i, far):
+            out = edit(roll(v, 1, 0), rows + REACH, lambda g: far)
+            out = edit(out, 0, lambda g: g + x_back(k, i))
+            if k >= chunks:
+                out = edit(out, rows, lambda g: g + x_corner(k, 4 + i))
             return out
 
-        zero = jnp.zeros((wide_rows, LANES), jnp.float32)
         for r in range(2):
-            def x_up(v, k, c):
-                out = roll(v, -1, 0) + at_row(rows - 1, x_ahead(k, 2 * r + c))
-                if k >= chunks:
-                    out = out + at_row(wide_rows - 1, x_corner(k, 2 * r + c))
-                return out
-
-            def x_down(v, k, c, far):
-                out = jnp.where(row_id == rows + REACH, far, roll(v, 1, 0))
-                out = out + at_row(0, x_back(k, 2 * r + c))
-                if k >= chunks:
-                    out = out + at_row(rows, x_corner(k, 4 + 2 * r + c))
-                return out
-
-            ex, ey, ez = get(r, 0), get(r, 1), get(r, 2)
-            got = keep_y_next * jnp.concatenate(
+            got = jnp.concatenate(
                 [
                     recv_c[n, 2 * r],
                     recv_c[n, 2 * r + 1],
@@ -527,22 +565,33 @@
                 axis=0,
             )
             corner = tall(pair(recv_a[n, 1], recv_b[n, 1], r))
-            y_ez = y_up(ez, got, corner)
-            y_ex = y_up(ex, roll(got, NZ, 1), roll(corner, NZ, 1))
-            for k in range(wide_chunks):
-                x_ez, x_ey = x_up(ez[k], k, 1), x_up(ey[k], k, 0)
-                z_ey = jnp.where(depth_last, 0.0, roll(ey[k], -1, 1))
-                z_ex = jnp.where(depth_last, 0.0, roll(ex[k], -1, 1))
-                curls = (
-                    (y_ez[k] - ez[k]) - (z_ey - ey[k]),
-                    (z_ex - ex[k]) - (x_ez - ez[k]),
-                    (x_ey - ey[k]) - (y_ex[k] - ex[k]),
-                )
-                for c in range(3):
-                    wide[r, 3 + c, :, part(k)] = wide[r, 3 + c, :, part(k)] - coefs[4, :, part(k)] * curls[c]
-
-            hx, hy, hz = get(r, 3), get(r, 4), get(r, 5)
-            got = keep_y_prev * jnp.concatenate(
+
+            def magnetic(ks):
+                turned_z, turned_x = Turned(r, 2), Turned(r, 0)
+                for k in ks:
+                    ex, ey, ez = (wide[r, c, :, part(k)] for c in range(3))
+                    y_ez = y_up(turned_z, k, got, corner)
+                    y_ex = y_up(turned_x, k, roll(got, NZ, 1), roll(corner, NZ, 1))
+                    x_ez, x_ey = x_up(ez, k, 2 * r + 1), x_up(ey, k, 2 * r)
+                    z_ey = jnp.where(depth_last, 0.0, roll(ey, -1, 1))
+                    z_ex = jnp.where(depth_last, 0.0, roll(ex, -1, 1))
+                    curls = (
+                        (y_ez - ez) - (z_ey - ey),
+                        (z_ex - ex) - (x_ez - ez),
+                        (x_ey - ey) - (y_ex - ex),
+                    )
+                    half_step = coefs[4, :, part(k)]
+                    for c in range(3):
+                        wide[r, 3 + c, :, part(k)] = wide[r, 3 + c, :, part(k)] - half_step * curls[c]
+
+            magnetic((wide_chunks - 1, *range(chunks + 1)))
+
+            @pl.when(n < 3)
+            def _():
+                magnetic((chunks + 1, chunks + 2))
+
+        for r in range(2):
+            got = jnp.concatenate(
                 [
                     recv_d[n, 2 * r],
                     recv_d[n, 2 * r + 1],
@@ -551,47 +600,56 @@
                 axis=0,
             )
             corner = tall(pair(recv_a[n, 2], recv_b[n, 2], r))
-            far_line = at_row(
-                rows - 1, (-time_step * start * keep_x_next) * roll(recv_back_up[0, 0, 4 + 2 * r : 5 + 2 * r], NZ, 1)
-            )
-            far_row = jnp.where(
-                low[0:1], 0.0, (time_step * start * keep_y_next) * roll(recv_ahead_down[0, 0, 4 * r + 3 : 4 * r + 4], NZ, 1)
-            )
-            y_hx = y_down(hx, got, corner, zero)
-            y_hz = y_down(hz, roll(got, NZ, 1), roll(corner, NZ, 1), far_line)
             amount = waveforms[0, r, n]
-            def electric(k):
-                x_hz = x_down(hz[k], k, 1, far_row if k == chunks - 1 else 0.0)
-                x_hy = x_down(hy[k], k, 0, 0.0)
-                z_hy = jnp.where(depth_first, 0.0, roll(hy[k], 1, 1))
-                z_hx = jnp.where(depth_first, 0.0, roll(hx[k], 1, 1))
-                curls = (
-                    (hz[k] - y_hz[k]) - (hy[k] - z_hy),
-                    (hx[k] - z_hx) - (hz[k] - x_hz),
-                    (hy[k] - x_hy) - (hx[k] - y_hx[k]),
-                )
-                for c in range(3):
-                    e = wide[r, c, :, part(k)]
-                    p = wide[r, 6 + c, :, part(k)]
-                    j = wide[r, 9 + c, :, part(k)]
-                    j = coefs[1, :, part(k)] * j + coefs[3, :, part(k)] * e - coefs[2, :, part(k)] * p
-                    wide[r, 9 + c, :, part(k)] = j
-                    wide[r, 6 + c, :, part(k)] = p + time_step * j
-                    new = e + coefs[0, :, part(k)] * (curls[c] - j)
-                    if k < chunks:
-                        new = new - amount * source[r, c, :, part(k)]
-                        if r == 0:
-                            moves[n, c, :, part(k)] = new[0:rows] - e[0:rows]
-                        else:
-                            duals[n, c, :, part(k)] = new[0:rows]
-                    wide[r, c, :, part(k)] = new
-            for k in range(chunks):
-                electric(k)
+
+            def electric(ks):
+                turned_x, turned_z = Turned(r, 3), Turned(r, 5)
+                for k in ks:
+                    hx, hy, hz = (wide[r, 3 + c, :, part(k)] for c in range(3))
+                    far_line, far_row = 0.0, jnp.zeros((1, LANES), jnp.float32)
+                    if k == chunks + chunks // 2:
+                        far = roll(recv_back_up[0, 0, 4 + 2 * r : 5 + 2 * r], NZ, 1)
+                        far_line = jnp.where(row_id == rows - 1, (-time_step * start) * far, 0.0)
+                    if k == chunks - 1:
+                        far = roll(recv_ahead_down[0, 0, 4 * r + 3 : 4 * r + 4], NZ, 1)
+                        far_row = jnp.where(low[0:1], 0.0, (time_step * start) * far)
+                    y_hx = y_down(turned_x, k, got, corner, 0.0)
+                    y_hz = y_down(turned_z, k, roll(got, NZ, 1), roll(corner, NZ, 1), far_line)
+                    x_hz = x_down(hz, k, 2 * r + 1, far_row)
+                    x_hy = x_down(hy, k, 2 * r, jnp.zeros((1, LANES), jnp.float32))
+                    z_hy = jnp.where(depth_first, 0.0, roll(hy, 1, 1))
+                    z_hx = jnp.where(depth_first, 0.0, roll(hx, 1, 1))
+                    curls = (
+                        (hz - y_hz) - (hy - z_hy),
+                        (hx - z_hx) - (hz - x_hz),
+                        (hy - x_hy) - (hx - y_hx),
+                    )
+                    reach, decay, drive, coupled = (coefs[i, :, part(k)] for i in range(4))
+                    for c in range(3):
+                        e = wide[r, c, :, part(k)]
+                        p = wide[r, 6 + c, :, part(k)]
+                        j = wide[r, 9 + c, :, part(k)]
+                        j = decay * j + coupled * e - drive * p
+                        wide[r, 9 + c, :, part(k)] = j
+                        wide[r, 6 + c, :, part(k)] = p + time_step * j
+                        new = e + reach * (curls[c] - j)
+                        if k < chunks:
+                            new = new - amount * source[r, c, :, part(k)]
+                            if r == 0:
+                                moves[n, c, :, part(k)] = new[0:rows] - e[0:rows]
+                            else:
+                                duals[n, c, :, part(k)] = new[0:rows]
+                        wide[r, c, :, part(k)] = new
+
+            electric(range(chunks))
 
             @pl.when(n < STEPS - 1)
             def _():
-                for k in range(chunks, wide_chunks):
-                    electric(k)
+                electric((chunks, wide_chunks - 1))
+
+            @pl.when(n < 2)
+            def _():
+                electric((chunks + 1, chunks + 2))
 
         return carry
 
@@ -622,10 +680,25 @@
                     value = value + duals[STEPS - 1 - i, c, :, part(k)] * moves[i, c, :, part(k)]
             partial[:, part(k)] = value
         swap[j].start()
+
+    @pl.when(far_half == 0)
+    def _():
+        pl.semaphore_wait(answer, 1)
+
     for j, p in enumerate(pieces):
         swap[j].wait_recv()
         half_sum[:, p] = partial[mine, p] + core_in[:, p]
         cross[j].start()
+    guarded(lambda copy: copy.wait_send(), medium_copies(), True)
+    for copy in shared_copies(core):
+        copy.wait_send()
+
+    def drain(n, carry):
+        guarded(lambda copy: copy.wait_send(), trace_copies(n), True)
+        return carry
+
+    lax.fori_loop(0, STEPS, drain, 0)
+
     for j, p in enumerate(pieces):
         cross[j].wait_recv()
         grad_out[mine, p] = (contrast * inside[mine, p]) * (half_sum[:, p] + chip_in[:, p])
@@ -635,14 +708,6 @@
     for copy in swap + cross + back:
         copy.wait_send()
 
-    for copy in medium_copies() + shared_copies(core):
-        copy.wait_send()
-
-    def drain(n, carry):
-        each_trace(n, lambda copy: copy.wait_send())
-        return carry
-
-    lax.fori_loop(0, STEPS, drain, 0)
     store.wait()
 
 
@@ -701,6 +766,7 @@
                 pltpu.SemaphoreType.DMA((3, 2)),
                 pltpu.SemaphoreType.DMA((10,)),
                 pltpu.SemaphoreType.DMA((2,)),
+                pltpu.SemaphoreType.REGULAR,
             ],
             compiler_params=pltpu.CompilerParams(collective_id=0, has_side_effects=True),
         )(fields, jnp.transpose(profiles, (0, 2, 1, 3)), waveforms, material_map, density, table, planes, box)

time: 38.7 us -> 32.2 us (0.83)
  the two profiles are of different devices: /device:TPU:1 before, /device:TPU:133 now
where the time goes in v4:
time: 32.2 us; the launch traced here: 32.1 us
  Pallas kernels  31.4 us (98%)
  between operations  0.64 us (2%)
    pallas_call x1, Pallas kernels, on_device(): pl.pallas_call(functools.partial(kernel, (n_wave, n_tx, n_ty, rows, flat)...  30.7 us
    pallas_call x1, Pallas kernels, on_device(): pl.pallas_call(put_out, out_shape=(jax.ShapeDtypeStruct((rows, flat), f32...  0.7 us

profile of v4, /device:TPU:133, one launch (start us, length us, event | category | flops | bytes accessed | tf_op | source)
XLA Modules:
  0.0 32.1 jit_solution(16523685338921694506)
XLA Ops:
  0.6 30.7 %shard_map.95 = (f32[16,512]{1,0:T(8,128)S(1)}, f32[1,2,3,16,512]{4,3,2,1,0:T(8,128)S(1)}) custom-call(f32[1,2,12,16,512]{4,3,2,1,0:T(8,128)} %fields.1, f32[1,3,2,8192]{3,2,1,0:T(2,128)} %bitcast.1, f32[1,2,5]{2,1,0:T(2,128)} %waveforms_in.1, s32[16,512]{1,0:T(8,128)} %material_in.1, f32[16,512]{1,0:T(8,128)} %density_in.1, f32[3,4]{1,0:T(4,128)} %table_in.1, ...), custom_call_target="tpu_custom_call" | custom-call | tf_op jit(solution)/shard_map/pallas_call | solution.py:734
  31.4 0.7 %shard_map.96 = (f32[16,512]{1,0:T(8,128)}, f32[1,2,3,16,512]{4,3,2,1,0:T(8,128)}) custom-call(f32[16,512]{1,0:T(8,128)S(1)} %get-tuple-element.4.grad, f32[1,2,3,16,512]{4,3,2,1,0:T(8,128)S(1)} %get-tuple-element.5.final), custom_call_target="tpu_custom_call" | custom-call | tf_op jit(solution)/shard_map/pallas_call | solution.py:773
